TPU v7x, 128 devices: a whole 4x4x4 slice. The times are simulated.
128 devices in a mesh: req: 32 (over y, x, core), mlp: 4 (over z).
Axes of the slice: x: 4, y: 4, z: 4, core: 2. Of those that a mesh axis runs over, the one named last changes fastest.
Arguments:
- tokens: bfloat16 [8192, 2560], P('req'), may hold values from -125 to 125
- lengths: int32 [32, 4], P('req'), may hold values from 1 to 128, 256 in all within a row
- page_table: int32 [32, 16], P('req'), may hold values from 0 to 15, each once within a row
- attn_norm: float32 [2560], replicated, may hold values from 0.25 to 1.75
- qkv_weight: bfloat16 [2560, 8, 768], P(None, 'mlp'), may hold values from -0.125 to 0.125
- q_norm: float32 [128], replicated, may hold values from 0.25 to 1.75
- k_norm: float32 [128], replicated, may hold values from 0.25 to 1.75
- o_weight: bfloat16 [4096, 2560], P('mlp'), may hold values from -0.09375 to 0.09375
- mlp_norm: float32 [2560], replicated, may hold values from 0.25 to 1.75
- gate_up: bfloat16 [9728, 2, 2560], P(('req', 'mlp')), may hold values from -0.125 to 0.125
- down_weight: bfloat16 [9728, 2560], P(('req', 'mlp')), may hold values from -0.0625 to 0.0625
Outputs:
- layer_out: bfloat16 [8192, 2560], P(('req', 'mlp'))
- kv_cache: bfloat16 [2, 512, 16, 8, 128], P(None, 'req', None, 'mlp')
Inputs may be any that keep to these rules, and one draw needn't show every extreme that they name: `lengths`: each row sums to 256, and the longest prompt of every pack is exactly 128. `page_table`: each row is a permutation of 0 .. 15.
All inputs are finite; a program needn't handle non-finite values.
Results may differ from a plain program's by a relative error of at most 0.0049.
Values may be sent and summed in bfloat16 or wider, within the bound.
No kernel may reach another device: no remote copies, remote signals or barrier semaphores. Data moves between devices by JAX's collectives and lax.ppermute only.
A program may use at most 128 MiB of HBM per device.

v0:
```python
import math

import jax
import jax.numpy as jnp
from jax import lax
from jax.experimental import pallas as pl
from jax.experimental.pallas import tpu as pltpu
from jax.sharding import PartitionSpec as P


rope_theta = 1000000.0
norm_eps = 1e-06

AXES = ("req", "mlp")

bf16 = jnp.bfloat16
f32 = jnp.float32
VMEM_LIMIT = 16 * 2**20
INTERPRET = False
WHOLE = pl.BlockSpec(memory_space=pltpu.VMEM)

FLIPS = {
    "ya": (1, 0, 0, 0),
    "yb": (3, 0, 0, 0),
    "xa": (0, 1, 0, 0),
    "xb": (0, 3, 0, 0),
    "za": (0, 0, 0, 1),
    "zb": (0, 0, 0, 3),
    "core": (0, 0, 1, 0),
}
CUBE = ("ya", "za", "yb", "zb")


def pairs(flip_core0, flip_core1):
    out = []
    for y in range(4):
        for x in range(4):
            for core in range(2):
                for z in range(4):
                    fy, fx, fc, fz = FLIPS[flip_core1 if core else flip_core0]
                    there = (y ^ fy, x ^ fx, core ^ fc, z ^ fz)
                    src = ((y * 4 + x) * 2 + core) * 4 + z
                    dst = ((there[0] * 4 + there[1]) * 2 + there[2]) * 4 + there[3]
                    out.append((src, dst))
    return out


def send(values, flip_core0, flip_core1):
    return lax.ppermute(values, AXES, pairs(flip_core0, flip_core1))


def cube_send(values, slot, step):
    return send(values, CUBE[(slot + step) % 4], CUBE[(2 + slot + step) % 4])


def rms_scale(values, gain):
    mean_sq = jnp.mean(values * values, axis=-1, keepdims=True)
    return values * lax.rsqrt(mean_sq + norm_eps) * gain


def attention(qkv, q_norm, k_norm, lengths, page_table, place):
    local_kv, slots, _ = qkv.shape
    head_dim = q_norm.shape[0]
    half = head_dim // 2
    group_q = qkv.shape[2] // head_dim - 2
    prompts = lengths.shape[1]
    pages = page_table.shape[1]
    page_rows = slots // pages
    owned = slots // 4
    freq = rope_theta ** (-(2.0 * jnp.arange(half, dtype=f32)) / head_dim)
    freq = jnp.concatenate([freq, freq])[None, :]

    def kernel(lengths_ref, pages_ref, place_ref, qkv_ref, q_ref, k_ref, freq_ref, ctx_ref, kv_ref):
        def segments(dim, shape):
            ids = lax.broadcasted_iota(jnp.int32, shape, dim)
            segment = jnp.zeros(shape, jnp.int32)
            start = jnp.zeros(shape, jnp.int32)
            end = jnp.int32(0)
            for p in range(prompts):
                end = end + lengths_ref[0, p]
                segment = segment + (ids >= end).astype(jnp.int32)
                start = jnp.where(ids >= end, end, start)
            return ids, segment, ids - start

        _, _, position = segments(0, (slots, head_dim))
        angle = position.astype(f32) * freq_ref[...]
        cosine = jnp.cos(angle)
        sine = jnp.sin(angle)
        lane = lax.broadcasted_iota(jnp.int32, (slots, head_dim), 1)
        sine = jnp.where(lane < half, -sine, sine)
        query_id, query_segment, _ = segments(0, (slots, slots))
        key_id, key_segment, _ = segments(1, (slots, slots))
        allowed = (query_segment == key_segment) & (key_id <= query_id)

        def headed(values, gain):
            mean_sq = jnp.mean(values * values, axis=-1, keepdims=True)
            values = values * lax.rsqrt(mean_sq + norm_eps) * gain
            return (values * cosine + pltpu.roll(values, half, 1) * sine).astype(bf16)

        def block_at(owner):
            apart = owner ^ place_ref[0, 0]
            at = jnp.where(apart == place_ref[0, 1], 0, 1)
            at = jnp.where(apart == 0, 2, at)
            at = jnp.where(apart == place_ref[0, 2], 3, at)
            return pl.multiple_of(at * owned, owned)

        targets = [block_at(owner) for owner in range(4)]
        homes = [pl.multiple_of(pages_ref[0, p] * page_rows, page_rows) for p in range(pages)]
        for j in range(local_kv):
            key = headed(qkv_ref[j, :, group_q * head_dim : (group_q + 1) * head_dim], k_ref[...])
            value = qkv_ref[j, :, (group_q + 1) * head_dim :].astype(bf16)
            for p in range(pages):
                kv_ref[0, j, pl.ds(homes[p], page_rows), :] = key[p * page_rows : (p + 1) * page_rows]
                kv_ref[1, j, pl.ds(homes[p], page_rows), :] = value[
                    p * page_rows : (p + 1) * page_rows
                ]
            for i in range(group_q):
                query = headed(qkv_ref[j, :, i * head_dim : (i + 1) * head_dim], q_ref[...])
                scores = lax.dot_general(
                    query, key, (((1,), (1,)), ((), ())), preferred_element_type=f32
                ) * (1.0 / math.sqrt(head_dim))
                weights = jnp.where(allowed, jnp.exp(scores), 0.0)
                probs = (weights / jnp.sum(weights, axis=-1, keepdims=True)).astype(bf16)
                context = jnp.dot(probs, value, preferred_element_type=f32).astype(bf16)
                at = (j * group_q + i) * head_dim
                for owner in range(4):
                    ctx_ref[pl.ds(targets[owner], owned), at : at + head_dim] = context[
                        owner * owned : (owner + 1) * owned
                    ]

    scalars = pl.BlockSpec(memory_space=pltpu.SMEM)
    return pl.pallas_call(
        kernel,
        out_shape=[
            jax.ShapeDtypeStruct((slots, local_kv * group_q * head_dim), bf16),
            jax.ShapeDtypeStruct((2, local_kv, slots, head_dim), bf16),
        ],
        in_specs=[scalars] * 3 + [WHOLE] * 4,
        out_specs=[WHOLE] * 2,
        compiler_params=pltpu.CompilerParams(vmem_limit_bytes=VMEM_LIMIT),
        interpret=INTERPRET,
    )(lengths, page_table, place, qkv, q_norm[None, :], k_norm[None, :], freq)


def starts_of(pieces):
    return [sum(p.shape[0] for p in pieces[:i]) for i in range(len(pieces) + 1)]


def feed_forward_body(ins, rows, gate_upper_ref, down_ref, outs):
    starts = starts_of(ins)
    units = down_ref.shape[0]
    for i, piece in enumerate(ins):
        rows[starts[i] : starts[i + 1], :] = piece[...]
    hidden = lax.dot_general(
        rows[...], gate_upper_ref[...], (((1,), (1,)), ((), ())), preferred_element_type=f32
    )
    gate, upper = hidden[:, :units], hidden[:, units:]
    act = (gate / (1.0 + jnp.exp(-gate)) * upper).astype(bf16)
    out = jnp.dot(act, down_ref[...], preferred_element_type=f32)
    for i, piece in enumerate(outs):
        piece[...] = out[starts[i] : starts[i + 1], :].astype(piece.dtype)


def feed_forward(pieces, gate_upper, down, out_types):
    count = len(pieces)

    def kernel(*refs):
        feed_forward_body(
            refs[:count], refs[-1], refs[count], refs[count + 1], refs[count + 2 : -1]
        )

    return pl.pallas_call(
        kernel,
        out_shape=[jax.ShapeDtypeStruct(p.shape, t) for p, t in zip(pieces, out_types)],
        in_specs=[WHOLE] * (count + 2),
        out_specs=[WHOLE] * count,
        scratch_shapes=[pltpu.VMEM((starts_of(pieces)[-1], down.shape[1]), bf16)],
        compiler_params=pltpu.CompilerParams(vmem_limit_bytes=VMEM_LIMIT),
        interpret=INTERPRET,
    )(*pieces, gate_upper, down)


def feed_forward_first(pieces, shards, out_types):
    count, parts = len(pieces), len(shards)
    each = shards[0].shape[0] // 3
    width = shards[0].shape[1]
    units = parts * each

    def kernel(*refs):
        ins, held, outs = refs[:count], refs[count : count + parts], refs[count + parts : -3]
        gate_upper_ref, down_ref, rows = refs[-3:]
        for i, shard in enumerate(held):
            gate_upper_ref[i * each : (i + 1) * each, :] = shard[:each, :]
            gate_upper_ref[units + i * each : units + (i + 1) * each, :] = shard[each : 2 * each, :]
            down_ref[i * each : (i + 1) * each, :] = shard[2 * each :, :]
        feed_forward_body(ins, rows, gate_upper_ref, down_ref, outs)

    shapes = [jax.ShapeDtypeStruct(p.shape, t) for p, t in zip(pieces, out_types)]
    shapes.append(jax.ShapeDtypeStruct((2 * units, width), bf16))
    shapes.append(jax.ShapeDtypeStruct((units, width), bf16))
    outs = pl.pallas_call(
        kernel,
        out_shape=shapes,
        in_specs=[WHOLE] * (count + parts),
        out_specs=[WHOLE] * (count + 2),
        scratch_shapes=[pltpu.VMEM((starts_of(pieces)[-1], width), bf16)],
        compiler_params=pltpu.CompilerParams(vmem_limit_bytes=VMEM_LIMIT),
        interpret=INTERPRET,
    )(*pieces, *shards)
    return outs[:-2], outs[-2], outs[-1]


def per_device(
    tokens,
    lengths,
    page_table,
    attn_norm,
    qkv_weight,
    q_norm,
    k_norm,
    o_weight,
    mlp_norm,
    gate_up,
    down_weight,
):
    slots = tokens.shape[0]
    head_dim = q_norm.shape[0]
    local_kv = qkv_weight.shape[1]
    pages = page_table.shape[1]
    page_rows = slots // pages
    owned = slots // 4
    core = lax.axis_index("req") % 2
    z = lax.axis_index("mlp")

    units = gate_up.shape[0]
    padded = -(-units // 16) * 16
    pad = ((0, padded - units), (0, 0))
    own = jnp.concatenate(
        [jnp.pad(gate_up[:, 0, :], pad), jnp.pad(gate_up[:, 1, :], pad), jnp.pad(down_weight, pad)]
    )
    own1 = send(own, "xa", "xb")
    own2 = send(own, "xb", "xa")
    own3 = send(own1, "xb", "xa")
    chip_half = [own, own1, own2, own3]
    shards = chip_half + [send(w, "core", "core") for w in chip_half]

    first = jnp.where(core == 0, 1, 3)
    second = jnp.where(core == 0, 3, 1)
    normed = rms_scale(tokens.astype(f32), attn_norm).astype(bf16)
    qkv = jnp.einsum("sd,dkc->ksc", normed, qkv_weight, preferred_element_type=f32)
    context, pages_out = attention(
        qkv, q_norm, k_norm, lengths, page_table, jnp.stack([z, first, second])[None, :]
    )
    kv_cache = pages_out.reshape(2, local_kv, pages, page_rows, head_dim)
    kv_cache = kv_cache.transpose(0, 2, 3, 1, 4)

    def rows_of(values, owner):
        return lax.dynamic_slice_in_dim(values, owner * owned, owned, 0)

    out_leaving = jnp.dot(context[: 2 * owned], o_weight, preferred_element_type=f32).astype(bf16)
    arrived = send(out_leaving, "za", "zb").astype(f32)
    out_staying = jnp.dot(context[2 * owned :], o_weight, preferred_element_type=f32)
    out_staying = lax.optimization_barrier(out_staying) + arrived
    arrived = send(out_staying[owned:].astype(bf16), "zb", "za").astype(f32)
    attn_out = out_staying[:owned] + arrived
    resid = rows_of(tokens, z).astype(f32) + attn_out
    mlp_in = rms_scale(resid, mlp_norm).astype(bf16)

    half = owned // 2
    even, odd = [], []
    for i in range(2):
        mine = mlp_in[i * half : (i + 1) * half]
        even.append(mine)
        odd.append(cube_send(mine, i, 0))
    for step in (1, 2):
        for i in range(2):
            count = even[i].shape[0]
            came = cube_send(jnp.concatenate([even[i], odd[i]]), i, step)
            even[i] = jnp.concatenate([even[i], came[:count]])
            odd[i] = jnp.concatenate([odd[i], came[count:]])
    far_odd, far_even = [], []
    for i in range(2):
        far_odd.append(cube_send(odd[i], i, 3))
    for i in range(2):
        far_even.append(cube_send(even[i], i, 3))

    outs, gate_upper, down = feed_forward_first(odd + even, shards, (bf16, bf16, f32, f32))
    *odd_out, even0, even1 = outs
    even_out = [even0, even1]
    far_odd_out = feed_forward(far_odd, gate_upper, down, (bf16, bf16))
    far_even_out = feed_forward(far_even, gate_upper, down, (f32, f32))

    total = []
    for i in range(2):
        near = even_out[i] + cube_send(odd_out[i], i, 0).astype(f32)
        far = far_even_out[i] + cube_send(far_odd_out[i], i, 0).astype(f32)
        total.append(near + cube_send(far.astype(bf16), i, 3).astype(f32))
    for step in (2, 1):
        for i in range(2):
            rows = total[i].shape[0] // 2
            total[i] = total[i][:rows] + cube_send(total[i][rows:].astype(bf16), i, step).astype(f32)
    layer_out = (resid + jnp.concatenate(total)).astype(bf16)
    return (layer_out, kv_cache)


def solution(mesh):
    return jax.shard_map(
        per_device,
        mesh=mesh,
        in_specs=(
            P("req", None),
            P("req", None),
            P("req", None),
            P(),
            P(None, "mlp", None),
            P(),
            P(),
            P("mlp", None),
            P(),
            P(("req", "mlp"), None, None),
            P(("req", "mlp"), None),
        ),
        out_specs=(P(("req", "mlp"), None), P(None, "req", None, "mlp", None)),
        check_vma=False,
    )
```

profile of v0, /device:TPU:0, one launch (start us, length us, event | category | flops | bytes accessed | tf_op | source)
XLA Modules:
  0.0 148.9 jit_solution(16646434771438827127)
XLA Ops:
  0.7 1.7 %fusion.2 = f32[256]{0:T(256)S(1)} fusion(bf16[256,2560]{1,0:T(8,128)(2,1)} %param.11), kind=kLoop, calls=%fused_computation.7 | loop fusion | flops 1965824 | bytes 1311744 | tf_op jit(solution)/shard_map/reduce_sum | solution.py:57
  2.7 5.6 %fusion.9.qkv_ref = f32[2,256,768]{2,1,0:T(8,128)S(1)} fusion(bf16[2560,2,768]{2,1,0:T(2,128)(2,1)} %param.15, bf16[256,2560]{1,0:T(8,128)(2,1)S(1)} %copy-done.6, f32[2560]{0:T(1024)S(1)} %copy-done.9, f32[256]{0:T(256)S(1)} %add_rsqrt_fusion), kind=kOutput, calls=%fused_computation.16 | convolution fusion | flops 2015887360 | bytes 10759168 | tf_op jit(solution)/shard_map/sd,dkc->ksc/dot_general | solution.py:250
  8.3 5.4 %shard_map.122 = (bf16[256,1024]{1,0:T(8,128)(2,1)S(1)}, bf16[2,2,256,128]{3,2,1,0:T(8,128)(2,1)S(1)}) custom-call(s32[1,4]{1,0:T(1,128)S(1)} %copy-done, s32[1,16]{1,0:T(1,128)S(1)} %copy-done.1, s32[1,3]{1,0:T(1,128)S(1)} %add_bitcast_fusion.place_ref, f32[2,256,768]{2,1,0:T(8,128)S(1)} %fusion.9.qkv_ref, f32[1,128]{1,0:T(1,128)S(1)} %bitcast.25, ...), custom_call_target="tpu_custom_call" | custom-call | tf_op jit(solution)/shard_map/pallas_call | solution.py:132
  13.8 0.9 convolution_convert_fusion
  14.7 2.1 %collective-permute-start = (bf16[128,2560]{1,0:T(8,128)(2,1)S(1)}, bf16[128,2560]{1,0:T(8,128)(2,1)S(1)}, u32[]{:S(2)}, u32[]{:S(2)}) collective-permute-start(bf16[128,2560]{1,0:T(8,128)(2,1)S(1)} %convolution_convert_fusion), channel_id=1, source_target_pairs={{0,1},{1,0},{2,3},{3,2},{4,7},{5,6},{6,5},{7,4},{8,9},{9,8},{10,11... | collective-permute-start | bytes 1966088 | tf_op jit(solution)/shard_map/ppermute | solution.py:49
  16.8 0.9 fusion.21
  17.7 1.1 fusion.24
  18.9 6.5 %collective-permute-done = bf16[128,2560]{1,0:T(8,128)(2,1)S(1)} collective-permute-done((bf16[128,2560]{1,0:T(8,128)(2,1)S(1)}, bf16[128,2560]{1,0:T(8,128)(2,1)S(1)}, u32[]{:S(2)}, u32[]{:S(2)}) %collective-permute-start) | collective-permute-done | bytes 655392 | tf_op jit(solution)/shard_map/ppermute | solution.py:49
  25.6 0.8 slice.139
  26.4 4.1 %collective-permute-start.1 = (bf16[64,2560]{1,0:T(8,128)(2,1)}, bf16[64,2560]{1,0:T(8,128)(2,1)}, u32[]{:S(2)}, u32[]{:S(2)}) collective-permute-start(bf16[64,2560]{1,0:T(8,128)(2,1)} %slice.139), channel_id=1, source_target_pairs={{0,3},{1,2},{2,1},{3,0},{4,5},{5,4},{6,7},{7,6},{8,11},{9,10},{10,... | collective-permute-start | bytes 983048 | tf_op jit(solution)/shard_map/ppermute | solution.py:49
  30.6 1.6 %collective-permute-start.8 = (bf16[240,2560]{1,0:T(8,128)(2,1)S(1)}, bf16[240,2560]{1,0:T(8,128)(2,1)S(1)}, u32[]{:S(2)}, u32[]{:S(2)}) collective-permute-start(bf16[240,2560]{1,0:T(8,128)(2,1)S(1)} %fusion.17.refs_4_), channel_id=1, source_target_pairs={{0,8},{1,9},{2,10},{3,11},{4,28},{5,29},{6,30},{7,31},{8,0},{9,1},... | collective-permute-start | bytes 3686408 | tf_op jit(solution)/shard_map/ppermute | solution.py:49
  32.2 2.1 %collective-permute-start.9 = (bf16[240,2560]{1,0:T(8,128)(2,1)S(1)}, bf16[240,2560]{1,0:T(8,128)(2,1)}, u32[]{:S(2)}, u32[]{:S(2)}) collective-permute-start(bf16[240,2560]{1,0:T(8,128)(2,1)S(1)} %fusion.17.refs_4_), channel_id=1, source_target_pairs={{0,24},{1,25},{2,26},{3,27},{4,12},{5,13},{6,14},{7,15},{8,16},{9,... | collective-permute-start | bytes 3686408 | tf_op jit(solution)/shard_map/ppermute | solution.py:49
  34.3 1.6 %collective-permute-done.1 = bf16[64,2560]{1,0:T(8,128)(2,1)} collective-permute-done((bf16[64,2560]{1,0:T(8,128)(2,1)}, bf16[64,2560]{1,0:T(8,128)(2,1)}, u32[]{:S(2)}, u32[]{:S(2)}) %collective-permute-start.1) | collective-permute-done | bytes 327712 | tf_op jit(solution)/shard_map/ppermute | solution.py:49
  35.9 1.5 %multiply_reduce_fusion = (f32[64]{0:T(128)S(1)}, f32[64,2560]{1,0:T(8,128)S(1)}) fusion(bf16[64,2560]{1,0:T(8,128)(2,1)} %collective-permute-done.1, f32[128,2560]{1,0:T(8,128)} %copy-done.4, bf16[256,2560]{1,0:T(8,128)(2,1)} %param.11, s32[]{:T(128)S(6)} %select_n.17), kind=kLoop, calls=%fused_computation.45 | loop fusion | flops 982976 | bytes 1966340 | tf_op jit(solution)/shard_map/reduce_sum | solution.py:57
  37.7 0.8 collective-permute-start.11
  38.4 1.6 %collective-permute-start.2 = (bf16[32,2560]{1,0:T(8,128)(2,1)S(1)}, bf16[32,2560]{1,0:T(8,128)(2,1)S(1)}, u32[]{:S(2)}, u32[]{:S(2)}) collective-permute-start(bf16[32,2560]{1,0:T(8,128)(2,1)S(1)} %get-tuple-element.37), channel_id=1, source_target_pairs={{0,32},{1,33},{2,34},{3,35},{4,100},{5,101},{6,102},{7,103},{8,40}... | collective-permute-start | bytes 491528 | tf_op jit(solution)/shard_map/ppermute | solution.py:49
  40.0 3.0 %collective-permute-done.5 = bf16[32,2560]{1,0:T(8,128)(2,1)S(1)} collective-permute-done((bf16[32,2560]{1,0:T(8,128)(2,1)S(1)}, bf16[32,2560]{1,0:T(8,128)(2,1)S(1)}, u32[]{:S(2)}, u32[]{:S(2)}) %collective-permute-start.5) | collective-permute-done | bytes 163872 | tf_op jit(solution)/shard_map/ppermute | solution.py:49
  43.0 3.1 %collective-permute-start.6 = (bf16[64,2560]{1,0:T(8,128)(2,1)S(1)}, bf16[64,2560]{1,0:T(8,128)(2,1)S(1)}, u32[]{:S(2)}, u32[]{:S(2)}) collective-permute-start(bf16[64,2560]{1,0:T(8,128)(2,1)S(1)} %pad_maximum_fusion.9), channel_id=1, source_target_pairs={{0,96},{1,97},{2,98},{3,99},{4,36},{5,37},{6,38},{7,39},{8,104},{9... | collective-permute-start | bytes 983048 | tf_op jit(solution)/shard_map/ppermute | solution.py:49
  46.2 14.4 %collective-permute-done.8.refs_5_ = bf16[240,2560]{1,0:T(8,128)(2,1)S(1)} collective-permute-done((bf16[240,2560]{1,0:T(8,128)(2,1)S(1)}, bf16[240,2560]{1,0:T(8,128)(2,1)S(1)}, u32[]{:S(2)}, u32[]{:S(2)}) %collective-permute-start.8) | collective-permute-done | bytes 1228832 | tf_op jit(solution)/shard_map/ppermute | solution.py:49
  60.6 0.5 collective-permute-start.13
  61.2 2.3 %collective-permute-start.7 = (bf16[128,2560]{1,0:T(8,128)(2,1)S(1)}, bf16[128,2560]{1,0:T(8,128)(2,1)S(1)}, u32[]{:S(2)}, u32[]{:S(2)}) collective-permute-start(bf16[128,2560]{1,0:T(8,128)(2,1)S(1)} %pad_maximum_fusion.3), channel_id=1, source_target_pairs={{0,3},{1,2},{2,1},{3,0},{4,5},{5,4},{6,7},{7,6},{8,11},{9,10},{10,... | collective-permute-start | bytes 1966088 | tf_op jit(solution)/shard_map/ppermute | solution.py:49
  63.6 9.5 %collective-permute-done.7 = bf16[128,2560]{1,0:T(8,128)(2,1)S(1)} collective-permute-done((bf16[128,2560]{1,0:T(8,128)(2,1)S(1)}, bf16[128,2560]{1,0:T(8,128)(2,1)S(1)}, u32[]{:S(2)}, u32[]{:S(2)}) %collective-permute-start.7) | collective-permute-done | bytes 655392 | tf_op jit(solution)/shard_map/ppermute | solution.py:49
  73.1 3.0 %collective-permute-start.4 = (bf16[128,2560]{1,0:T(8,128)(2,1)S(1)}, bf16[128,2560]{1,0:T(8,128)(2,1)S(1)}, u32[]{:S(2)}, u32[]{:S(2)}) collective-permute-start(bf16[128,2560]{1,0:T(8,128)(2,1)S(1)} %pad_maximum_fusion), channel_id=1, source_target_pairs={{0,96},{1,97},{2,98},{3,99},{4,36},{5,37},{6,38},{7,39},{8,104},{9... | collective-permute-start | bytes 1966088 | tf_op jit(solution)/shard_map/ppermute | solution.py:49
  76.2 8.9 %collective-permute-done.4 = bf16[128,2560]{1,0:T(8,128)(2,1)S(1)} collective-permute-done((bf16[128,2560]{1,0:T(8,128)(2,1)S(1)}, bf16[128,2560]{1,0:T(8,128)(2,1)S(1)}, u32[]{:S(2)}, u32[]{:S(2)}) %collective-permute-start.4) | collective-permute-done | bytes 655392 | tf_op jit(solution)/shard_map/ppermute | solution.py:49
  85.1 0.4 collective-permute-start.19
  85.6 2.3 %collective-permute-start.18 = (bf16[128,2560]{1,0:T(8,128)(2,1)S(1)}, bf16[128,2560]{1,0:T(8,128)(2,1)S(1)}, u32[]{:S(2)}, u32[]{:S(2)}) collective-permute-start(bf16[128,2560]{1,0:T(8,128)(2,1)S(1)} %pad_maximum_fusion.2.refs_0_), channel_id=1, source_target_pairs={{0,3},{1,2},{2,1},{3,0},{4,5},{5,4},{6,7},{7,6},{8,11},{9,10},{10,... | collective-permute-start | bytes 1966088 | tf_op jit(solution)/shard_map/ppermute | solution.py:49
  88.1 1.7 %collective-permute-start.17 = (bf16[128,2560]{1,0:T(8,128)(2,1)S(1)}, bf16[128,2560]{1,0:T(8,128)(2,1)S(1)}, u32[]{:S(2)}, u32[]{:S(2)}) collective-permute-start(bf16[128,2560]{1,0:T(8,128)(2,1)S(1)} %pad_maximum_fusion.7.refs_3_), channel_id=1, source_target_pairs={{0,32},{1,33},{2,34},{3,35},{4,100},{5,101},{6,102},{7,103},{8,40}... | collective-permute-start | bytes 1966088 | tf_op jit(solution)/shard_map/ppermute | solution.py:49
  89.7 1.0 collective-permute-start.16
  90.7 8.4 %shard_map.123 = (bf16[128,2560]{1,0:T(8,128)(2,1)S(1)}, bf16[128,2560]{1,0:T(8,128)(2,1)S(1)}, f32[128,2560]{1,0:T(8,128)S(1)}, f32[128,2560]{1,0:T(8,128)S(1)}...) custom-call(bf16[128,2560]{1,0:T(8,128)(2,1)S(1)} %pad_maximum_fusion.2.refs_0_, ...), custom_call_target="tpu_custom_call" | custom-call | tf_op jit(solution)/shard_map/pallas_call | solution.py:201
  99.1 3.7 %shard_map.125 = (bf16[128,2560]{1,0:T(8,128)(2,1)S(1)}, bf16[128,2560]{1,0:T(8,128)(2,1)S(1)}) custom-call(bf16[128,2560]{1,0:T(8,128)(2,1)S(1)} %collective-permute-done.18.refs_0_, bf16[128,2560]{1,0:T(8,128)(2,1)S(1)} %collective-permute-done.19.refs_1_, bf16[1280,2560]{1,0:T(8,128)(2,1)S(1)} %get-tuple-element.17.refs_2_, ...), custom_call_target="tpu_custom_call" | custom-call | tf_op jit(solution)/shard_map/pallas_call | solution.py:172
  102.8 0.5 collective-permute-start.20
  103.3 1.0 copy.26
  104.3 1.6 %collective-permute-start.15 = (bf16[128,2560]{1,0:T(8,128)(2,1)S(1)}, bf16[128,2560]{1,0:T(8,128)(2,1)S(1)}, u32[]{:S(2)}, u32[]{:S(2)}) collective-permute-start(bf16[128,2560]{1,0:T(8,128)(2,1)S(1)} %get-tuple-element.16), channel_id=1, source_target_pairs={{0,32},{1,33},{2,34},{3,35},{4,100},{5,101},{6,102},{7,103},{8,40}... | collective-permute-start | bytes 1966088 | tf_op jit(solution)/shard_map/ppermute | solution.py:49
  105.9 2.0 %collective-permute-start.24 = (bf16[128,2560]{1,0:T(8,128)(2,1)S(1)}, bf16[128,2560]{1,0:T(8,128)(2,1)S(1)}, u32[]{:S(2)}, u32[]{:S(2)}) collective-permute-start(bf16[128,2560]{1,0:T(8,128)(2,1)S(1)} %get-tuple-element.22), channel_id=1, source_target_pairs={{0,1},{1,0},{2,3},{3,2},{4,7},{5,6},{6,5},{7,4},{8,9},{9,8},{10,11... | collective-permute-start | bytes 1966088 | tf_op jit(solution)/shard_map/ppermute | solution.py:49
  108.0 3.7 %shard_map.124 = (f32[128,2560]{1,0:T(8,128)S(1)}, f32[128,2560]{1,0:T(8,128)S(1)}) custom-call(bf16[128,2560]{1,0:T(8,128)(2,1)S(1)} %collective-permute-done.16.refs_0_, bf16[128,2560]{1,0:T(8,128)(2,1)S(1)} %collective-permute-done.17.refs_1_, bf16[1280,2560]{1,0:T(8,128)(2,1)S(1)} %get-tuple-element.17.refs_2_, ...), custom_call_target="tpu_custom_call" | custom-call | tf_op jit(solution)/shard_map/pallas_call | solution.py:172
  111.7 1.8 %collective-permute-done.20 = bf16[128,2560]{1,0:T(8,128)(2,1)S(1)} collective-permute-done((bf16[128,2560]{1,0:T(8,128)(2,1)S(1)}, bf16[128,2560]{1,0:T(8,128)(2,1)S(1)}, u32[]{:S(2)}, u32[]{:S(2)}) %collective-permute-start.20) | collective-permute-done | bytes 655392 | tf_op jit(solution)/shard_map/ppermute | solution.py:49
  113.7 2.3 %collective-permute-start.21 = (bf16[128,2560]{1,0:T(8,128)(2,1)S(1)}, bf16[128,2560]{1,0:T(8,128)(2,1)S(1)}, u32[]{:S(2)}, u32[]{:S(2)}) collective-permute-start(bf16[128,2560]{1,0:T(8,128)(2,1)S(1)} %add_convert_fusion.1), channel_id=1, source_target_pairs={{0,3},{1,2},{2,1},{3,0},{4,5},{5,4},{6,7},{7,6},{8,11},{9,10},{10,... | collective-permute-start | bytes 1966088 | tf_op jit(solution)/shard_map/ppermute | solution.py:49
  116.0 1.1 collective-permute-done.25
  117.2 0.4 collective-permute-start.26
  117.6 2.9 %collective-permute-done.15 = bf16[128,2560]{1,0:T(8,128)(2,1)S(1)} collective-permute-done((bf16[128,2560]{1,0:T(8,128)(2,1)S(1)}, bf16[128,2560]{1,0:T(8,128)(2,1)S(1)}, u32[]{:S(2)}, u32[]{:S(2)}) %collective-permute-start.15) | collective-permute-done | bytes 655392 | tf_op jit(solution)/shard_map/ppermute | solution.py:49
  120.5 10.4 %collective-permute-done.21 = bf16[128,2560]{1,0:T(8,128)(2,1)S(1)} collective-permute-done((bf16[128,2560]{1,0:T(8,128)(2,1)S(1)}, bf16[128,2560]{1,0:T(8,128)(2,1)S(1)}, u32[]{:S(2)}, u32[]{:S(2)}) %collective-permute-start.21) | collective-permute-done | bytes 655392 | tf_op jit(solution)/shard_map/ppermute | solution.py:49
  131.2 1.0 collective-permute-start.22
  132.5 2.3 %collective-permute-start.27 = (bf16[64,2560]{1,0:T(8,128)(2,1)S(1)}, bf16[64,2560]{1,0:T(8,128)(2,1)S(1)}, u32[]{:S(2)}, u32[]{:S(2)}) collective-permute-start(bf16[64,2560]{1,0:T(8,128)(2,1)S(1)} %slice.137), channel_id=1, source_target_pairs={{0,3},{1,2},{2,1},{3,0},{4,5},{5,4},{6,7},{7,6},{8,11},{9,10},{10,... | collective-permute-start | bytes 983048 | tf_op jit(solution)/shard_map/ppermute | solution.py:49
  134.8 4.7 %collective-permute-done.22 = bf16[64,2560]{1,0:T(8,128)(2,1)S(1)} collective-permute-done((bf16[64,2560]{1,0:T(8,128)(2,1)S(1)}, bf16[64,2560]{1,0:T(8,128)(2,1)S(1)}, u32[]{:S(2)}, u32[]{:S(2)}) %collective-permute-start.22) | collective-permute-done | bytes 327712 | tf_op jit(solution)/shard_map/ppermute | solution.py:49
  139.7 1.3 collective-permute-done.27
  141.2 3.6 %collective-permute-start.28 = (bf16[32,2560]{1,0:T(8,128)(2,1)S(1)}, bf16[32,2560]{1,0:T(8,128)(2,1)S(1)}, u32[]{:S(2)}, u32[]{:S(2)}) collective-permute-start(bf16[32,2560]{1,0:T(8,128)(2,1)S(1)} %slice.140), channel_id=1, source_target_pairs={{0,96},{1,97},{2,98},{3,99},{4,36},{5,37},{6,38},{7,39},{8,104},{9... | collective-permute-start | bytes 491528 | tf_op jit(solution)/shard_map/ppermute | solution.py:49
  145.1 3.0 %collective-permute-done.28 = bf16[32,2560]{1,0:T(8,128)(2,1)S(1)} collective-permute-done((bf16[32,2560]{1,0:T(8,128)(2,1)S(1)}, bf16[32,2560]{1,0:T(8,128)(2,1)S(1)}, u32[]{:S(2)}, u32[]{:S(2)}) %collective-permute-start.28) | collective-permute-done | bytes 163872 | tf_op jit(solution)/shard_map/ppermute | solution.py:49
  148.1 0.8 fusion.19
  (82 shorter events, 2.7 us)
Async XLA Ops:
  0.6 2.0 %copy-start.6 = (bf16[256,2560]{1,0:T(8,128)(2,1)S(1)}, bf16[256,2560]{1,0:T(8,128)(2,1)}, u32[]{:S(2)}) copy-start(bf16[256,2560]{1,0:T(8,128)(2,1)} %param.11) | copy-start | bytes 3932164
  0.6 2.0 %copy-start.9 = (f32[2560]{0:T(1024)S(1)}, f32[2560]{0:T(1024)}, u32[]{:S(2)}) copy-start(f32[2560]{0:T(1024)} %param.14) | copy-start | bytes 30724
  2.5 11.3 %slice-start = ((s8[5242880]{0:T(1024)(128)(4,1)}), s8[4194304]{0:T(1024)(128)(4,1)S(1)}, s32[]{:S(2)}) async-start(s8[5242880]{0:T(1024)(128)(4,1)} %bitcast.27), calls=%async_computation | async-start | bytes 8388608
  2.6 5.7 %copy-start = (s32[1,4]{1,0:T(1,128)S(1)}, s32[1,4]{1,0:T(1,128)}, u32[]{:S(2)}) copy-start(s32[1,4]{1,0:T(1,128)} %lengths_ref.1) | copy-start | bytes 52
  2.6 5.7 %copy-start.1 = (s32[1,16]{1,0:T(1,128)S(1)}, s32[1,16]{1,0:T(1,128)}, u32[]{:S(2)}) copy-start(s32[1,16]{1,0:T(1,128)} %pages_ref.1) | copy-start | bytes 196
  2.6 5.7 %copy-start.2 = (f32[128]{0:T(128)S(1)}, f32[128]{0:T(128)}, u32[]{:S(2)}) copy-start(f32[128]{0:T(128)} %param.16) | copy-start | bytes 1540
  2.6 5.7 %copy-start.3 = (f32[128]{0:T(128)S(1)}, f32[128]{0:T(128)}, u32[]{:S(2)}) copy-start(f32[128]{0:T(128)} %param.17) | copy-start | bytes 1540
  2.6 11.1 %slice-start.1 = ((s8[5242880]{0:T(1024)(128)(4,1)}), s8[1048576]{0:T(1024)(128)(4,1)S(1)}, s32[]{:S(2)}) async-start(s8[5242880]{0:T(1024)(128)(4,1)} %bitcast.27), calls=%async_computation.1 | async-start | bytes 2097152
  14.7 3.0 %copy-start.5 = (bf16[76,2,2560]{2,1,0:T(2,128)(2,1)S(1)}, bf16[76,2,2560]{2,1,0:T(2,128)(2,1)}, u32[]{:S(2)}) copy-start(bf16[76,2,2560]{2,1,0:T(2,128)(2,1)} %param.20) | copy-start | bytes 2334724
  14.7 10.7 %collective-permute-start = (bf16[128,2560]{1,0:T(8,128)(2,1)S(1)}, bf16[128,2560]{1,0:T(8,128)(2,1)S(1)}, u32[]{:S(2)}, u32[]{:S(2)}) collective-permute-start(bf16[128,2560]{1,0:T(8,128)(2,1)S(1)} %convolution_convert_fusion), channel_id=1, source_target_pairs={{0,1},{1,0},{2,3},{3,2},{4,7},{5,6},{6,5},{7,4},{8,9},{9,8},{10,11... | collective-permute-start | bytes 1966088 | tf_op jit(solution)/shard_map/ppermute | solution.py:49
  18.9 11.6 %copy-start.7 = (bf16[76,2560]{1,0:T(8,128)(2,1)S(1)}, bf16[76,2560]{1,0:T(8,128)(2,1)}, u32[]{:S(2)}) copy-start(bf16[76,2560]{1,0:T(8,128)(2,1)} %param.21) | copy-start | bytes 1167364
  25.5 5.0 %copy-start.4 = (f32[128,2560]{1,0:T(8,128)}, f32[128,2560]{1,0:T(8,128)S(1)}, u32[]{:S(2)}) copy-start(f32[128,2560]{1,0:T(8,128)S(1)} %convert_add_fusion.2) | copy-start | bytes 3932164
  26.4 9.5 %collective-permute-start.1 = (bf16[64,2560]{1,0:T(8,128)(2,1)}, bf16[64,2560]{1,0:T(8,128)(2,1)}, u32[]{:S(2)}, u32[]{:S(2)}) collective-permute-start(bf16[64,2560]{1,0:T(8,128)(2,1)} %slice.139), channel_id=1, source_target_pairs={{0,3},{1,2},{2,1},{3,0},{4,5},{5,4},{6,7},{7,6},{8,11},{9,10},{10,... | collective-permute-start | bytes 983048 | tf_op jit(solution)/shard_map/ppermute | solution.py:49
  30.6 6.8 %copy-start.8 = (f32[2560]{0:T(1024)S(1)}, f32[2560]{0:T(1024)}, u32[]{:S(2)}) copy-start(f32[2560]{0:T(1024)} %param.19) | copy-start | bytes 30724
  30.6 30.0 %collective-permute-start.8 = (bf16[240,2560]{1,0:T(8,128)(2,1)S(1)}, bf16[240,2560]{1,0:T(8,128)(2,1)S(1)}, u32[]{:S(2)}, u32[]{:S(2)}) collective-permute-start(bf16[240,2560]{1,0:T(8,128)(2,1)S(1)} %fusion.17.refs_4_), channel_id=1, source_target_pairs={{0,8},{1,9},{2,10},{3,11},{4,28},{5,29},{6,30},{7,31},{8,0},{9,1},... | collective-permute-start | bytes 3686408 | tf_op jit(solution)/shard_map/ppermute | solution.py:49
  32.2 28.4 %collective-permute-start.9 = (bf16[240,2560]{1,0:T(8,128)(2,1)S(1)}, bf16[240,2560]{1,0:T(8,128)(2,1)}, u32[]{:S(2)}, u32[]{:S(2)}) collective-permute-start(bf16[240,2560]{1,0:T(8,128)(2,1)S(1)} %fusion.17.refs_4_), channel_id=1, source_target_pairs={{0,24},{1,25},{2,26},{3,27},{4,12},{5,13},{6,14},{7,15},{8,16},{9,... | collective-permute-start | bytes 3686408 | tf_op jit(solution)/shard_map/ppermute | solution.py:49
  37.6 5.4 %collective-permute-start.5 = (bf16[32,2560]{1,0:T(8,128)(2,1)S(1)}, bf16[32,2560]{1,0:T(8,128)(2,1)S(1)}, u32[]{:S(2)}, u32[]{:S(2)}) collective-permute-start(bf16[32,2560]{1,0:T(8,128)(2,1)S(1)} %get-tuple-element.36), channel_id=1, source_target_pairs={{0,1},{1,0},{2,3},{3,2},{4,7},{5,6},{6,5},{7,4},{8,9},{9,8},{10,11... | collective-permute-start | bytes 491528 | tf_op jit(solution)/shard_map/ppermute | solution.py:49
  37.7 47.9 %collective-permute-start.11 = (bf16[240,2560]{1,0:T(8,128)(2,1)S(1)}, bf16[240,2560]{1,0:T(8,128)(2,1)S(1)}, u32[]{:S(2)}, u32[]{:S(2)}) collective-permute-start(bf16[240,2560]{1,0:T(8,128)(2,1)S(1)} %fusion.17.refs_4_), channel_id=1, source_target_pairs={{0,4},{1,5},{2,6},{3,7},{4,0},{5,1},{6,2},{7,3},{8,12},{9,13},{10,... | collective-permute-start | bytes 3686408 | tf_op jit(solution)/shard_map/ppermute | solution.py:49
  38.4 7.7 %collective-permute-start.2 = (bf16[32,2560]{1,0:T(8,128)(2,1)S(1)}, bf16[32,2560]{1,0:T(8,128)(2,1)S(1)}, u32[]{:S(2)}, u32[]{:S(2)}) collective-permute-start(bf16[32,2560]{1,0:T(8,128)(2,1)S(1)} %get-tuple-element.37), channel_id=1, source_target_pairs={{0,32},{1,33},{2,34},{3,35},{4,100},{5,101},{6,102},{7,103},{8,40}... | collective-permute-start | bytes 491528 | tf_op jit(solution)/shard_map/ppermute | solution.py:49
  43.0 17.6 %collective-permute-start.6 = (bf16[64,2560]{1,0:T(8,128)(2,1)S(1)}, bf16[64,2560]{1,0:T(8,128)(2,1)S(1)}, u32[]{:S(2)}, u32[]{:S(2)}) collective-permute-start(bf16[64,2560]{1,0:T(8,128)(2,1)S(1)} %pad_maximum_fusion.9), channel_id=1, source_target_pairs={{0,96},{1,97},{2,98},{3,99},{4,36},{5,37},{6,38},{7,39},{8,104},{9... | collective-permute-start | bytes 983048 | tf_op jit(solution)/shard_map/ppermute | solution.py:49
  46.1 15.1 %collective-permute-start.3 = (bf16[64,2560]{1,0:T(8,128)(2,1)S(1)}, bf16[64,2560]{1,0:T(8,128)(2,1)S(1)}, u32[]{:S(2)}, u32[]{:S(2)}) collective-permute-start(bf16[64,2560]{1,0:T(8,128)(2,1)S(1)} %pad_maximum_fusion.8), channel_id=1, source_target_pairs={{0,1},{1,0},{2,3},{3,2},{4,7},{5,6},{6,5},{7,4},{8,9},{9,8},{10,11... | collective-permute-start | bytes 983048 | tf_op jit(solution)/shard_map/ppermute | solution.py:49
  60.6 24.9 %collective-permute-start.10 = (bf16[240,2560]{1,0:T(8,128)(2,1)S(1)}, bf16[240,2560]{1,0:T(8,128)(2,1)S(1)}, u32[]{:S(2)}, u32[]{:S(2)}) collective-permute-start(bf16[240,2560]{1,0:T(8,128)(2,1)S(1)} %collective-permute-done.8.refs_5_), channel_id=1, source_target_pairs={{0,24},{1,25},{2,26},{3,27},{4,12},{5,13},{6,14},{7,15},{8,16},{9,... | collective-permute-start | bytes 3686408 | tf_op jit(solution)/shard_map/ppermute | solution.py:49
  60.6 27.4 %collective-permute-start.12 = (bf16[240,2560]{1,0:T(8,128)(2,1)S(1)}, bf16[240,2560]{1,0:T(8,128)(2,1)S(1)}, u32[]{:S(2)}, u32[]{:S(2)}) collective-permute-start(bf16[240,2560]{1,0:T(8,128)(2,1)S(1)} %collective-permute-done.8.refs_5_), channel_id=1, source_target_pairs={{0,4},{1,5},{2,6},{3,7},{4,0},{5,1},{6,2},{7,3},{8,12},{9,13},{10,... | collective-permute-start | bytes 3686408 | tf_op jit(solution)/shard_map/ppermute | solution.py:49
  60.6 29.1 %collective-permute-start.13 = (bf16[240,2560]{1,0:T(8,128)(2,1)}, bf16[240,2560]{1,0:T(8,128)(2,1)S(1)}, u32[]{:S(2)}, u32[]{:S(2)}) collective-permute-start(bf16[240,2560]{1,0:T(8,128)(2,1)} %collective-permute-done.9.refs_6_), channel_id=1, source_target_pairs={{0,4},{1,5},{2,6},{3,7},{4,0},{5,1},{6,2},{7,3},{8,12},{9,13},{10,... | collective-permute-start | bytes 3686408 | tf_op jit(solution)/shard_map/ppermute | solution.py:49
  61.2 11.9 %collective-permute-start.7 = (bf16[128,2560]{1,0:T(8,128)(2,1)S(1)}, bf16[128,2560]{1,0:T(8,128)(2,1)S(1)}, u32[]{:S(2)}, u32[]{:S(2)}) collective-permute-start(bf16[128,2560]{1,0:T(8,128)(2,1)S(1)} %pad_maximum_fusion.3), channel_id=1, source_target_pairs={{0,3},{1,2},{2,1},{3,0},{4,5},{5,4},{6,7},{7,6},{8,11},{9,10},{10,... | collective-permute-start | bytes 1966088 | tf_op jit(solution)/shard_map/ppermute | solution.py:49
  73.1 12.0 %collective-permute-start.4 = (bf16[128,2560]{1,0:T(8,128)(2,1)S(1)}, bf16[128,2560]{1,0:T(8,128)(2,1)S(1)}, u32[]{:S(2)}, u32[]{:S(2)}) collective-permute-start(bf16[128,2560]{1,0:T(8,128)(2,1)S(1)} %pad_maximum_fusion), channel_id=1, source_target_pairs={{0,96},{1,97},{2,98},{3,99},{4,36},{5,37},{6,38},{7,39},{8,104},{9... | collective-permute-start | bytes 1966088 | tf_op jit(solution)/shard_map/ppermute | solution.py:49
  85.1 14.0 %collective-permute-start.19 = (bf16[128,2560]{1,0:T(8,128)(2,1)S(1)}, bf16[128,2560]{1,0:T(8,128)(2,1)S(1)}, u32[]{:S(2)}, u32[]{:S(2)}) collective-permute-start(bf16[128,2560]{1,0:T(8,128)(2,1)S(1)} %pad_maximum_fusion.5.refs_1_), channel_id=1, source_target_pairs={{0,32},{1,33},{2,34},{3,35},{4,100},{5,101},{6,102},{7,103},{8,40}... | collective-permute-start | bytes 1966088 | tf_op jit(solution)/shard_map/ppermute | solution.py:49
  85.5 5.2 %collective-permute-start.14 = (bf16[240,2560]{1,0:T(8,128)(2,1)S(1)}, bf16[240,2560]{1,0:T(8,128)(2,1)S(1)}, u32[]{:S(2)}, u32[]{:S(2)}) collective-permute-start(bf16[240,2560]{1,0:T(8,128)(2,1)S(1)} %collective-permute-done.10.refs_7_), channel_id=1, source_target_pairs={{0,4},{1,5},{2,6},{3,7},{4,0},{5,1},{6,2},{7,3},{8,12},{9,13},{10,... | collective-permute-start | bytes 3686408 | tf_op jit(solution)/shard_map/ppermute | solution.py:49
  85.6 13.5 %collective-permute-start.18 = (bf16[128,2560]{1,0:T(8,128)(2,1)S(1)}, bf16[128,2560]{1,0:T(8,128)(2,1)S(1)}, u32[]{:S(2)}, u32[]{:S(2)}) collective-permute-start(bf16[128,2560]{1,0:T(8,128)(2,1)S(1)} %pad_maximum_fusion.2.refs_0_), channel_id=1, source_target_pairs={{0,3},{1,2},{2,1},{3,0},{4,5},{5,4},{6,7},{7,6},{8,11},{9,10},{10,... | collective-permute-start | bytes 1966088 | tf_op jit(solution)/shard_map/ppermute | solution.py:49
  88.1 17.9 %collective-permute-start.17 = (bf16[128,2560]{1,0:T(8,128)(2,1)S(1)}, bf16[128,2560]{1,0:T(8,128)(2,1)S(1)}, u32[]{:S(2)}, u32[]{:S(2)}) collective-permute-start(bf16[128,2560]{1,0:T(8,128)(2,1)S(1)} %pad_maximum_fusion.7.refs_3_), channel_id=1, source_target_pairs={{0,32},{1,33},{2,34},{3,35},{4,100},{5,101},{6,102},{7,103},{8,40}... | collective-permute-start | bytes 1966088 | tf_op jit(solution)/shard_map/ppermute | solution.py:49
  89.7 18.2 %collective-permute-start.16 = (bf16[128,2560]{1,0:T(8,128)(2,1)S(1)}, bf16[128,2560]{1,0:T(8,128)(2,1)S(1)}, u32[]{:S(2)}, u32[]{:S(2)}) collective-permute-start(bf16[128,2560]{1,0:T(8,128)(2,1)S(1)} %pad_maximum_fusion.6.refs_2_), channel_id=1, source_target_pairs={{0,3},{1,2},{2,1},{3,0},{4,5},{5,4},{6,7},{7,6},{8,11},{9,10},{10,... | collective-permute-start | bytes 1966088 | tf_op jit(solution)/shard_map/ppermute | solution.py:49
  102.8 10.7 %collective-permute-start.20 = (bf16[128,2560]{1,0:T(8,128)(2,1)S(1)}, bf16[128,2560]{1,0:T(8,128)(2,1)S(1)}, u32[]{:S(2)}, u32[]{:S(2)}) collective-permute-start(bf16[128,2560]{1,0:T(8,128)(2,1)S(1)} %get-tuple-element.20), channel_id=1, source_target_pairs={{0,32},{1,33},{2,34},{3,35},{4,100},{5,101},{6,102},{7,103},{8,40}... | collective-permute-start | bytes 1966088 | tf_op jit(solution)/shard_map/ppermute | solution.py:49
  104.3 16.2 %collective-permute-start.15 = (bf16[128,2560]{1,0:T(8,128)(2,1)S(1)}, bf16[128,2560]{1,0:T(8,128)(2,1)S(1)}, u32[]{:S(2)}, u32[]{:S(2)}) collective-permute-start(bf16[128,2560]{1,0:T(8,128)(2,1)S(1)} %get-tuple-element.16), channel_id=1, source_target_pairs={{0,32},{1,33},{2,34},{3,35},{4,100},{5,101},{6,102},{7,103},{8,40}... | collective-permute-start | bytes 1966088 | tf_op jit(solution)/shard_map/ppermute | solution.py:49
  105.9 11.2 %collective-permute-start.25 = (bf16[128,2560]{1,0:T(8,128)(2,1)S(1)}, bf16[128,2560]{1,0:T(8,128)(2,1)S(1)}, u32[]{:S(2)}, u32[]{:S(2)}) collective-permute-start(bf16[128,2560]{1,0:T(8,128)(2,1)S(1)} %get-tuple-element.24), channel_id=1, source_target_pairs={{0,1},{1,0},{2,3},{3,2},{4,7},{5,6},{6,5},{7,4},{8,9},{9,8},{10,11... | collective-permute-start | bytes 1966088 | tf_op jit(solution)/shard_map/ppermute | solution.py:49
  105.9 26.3 %collective-permute-start.24 = (bf16[128,2560]{1,0:T(8,128)(2,1)S(1)}, bf16[128,2560]{1,0:T(8,128)(2,1)S(1)}, u32[]{:S(2)}, u32[]{:S(2)}) collective-permute-start(bf16[128,2560]{1,0:T(8,128)(2,1)S(1)} %get-tuple-element.22), channel_id=1, source_target_pairs={{0,1},{1,0},{2,3},{3,2},{4,7},{5,6},{6,5},{7,4},{8,9},{9,8},{10,11... | collective-permute-start | bytes 1966088 | tf_op jit(solution)/shard_map/ppermute | solution.py:49
  113.7 17.3 %collective-permute-start.21 = (bf16[128,2560]{1,0:T(8,128)(2,1)S(1)}, bf16[128,2560]{1,0:T(8,128)(2,1)S(1)}, u32[]{:S(2)}, u32[]{:S(2)}) collective-permute-start(bf16[128,2560]{1,0:T(8,128)(2,1)S(1)} %add_convert_fusion.1), channel_id=1, source_target_pairs={{0,3},{1,2},{2,1},{3,0},{4,5},{5,4},{6,7},{7,6},{8,11},{9,10},{10,... | collective-permute-start | bytes 1966088 | tf_op jit(solution)/shard_map/ppermute | solution.py:49
  117.2 15.0 %collective-permute-start.26 = (bf16[128,2560]{1,0:T(8,128)(2,1)S(1)}, bf16[128,2560]{1,0:T(8,128)(2,1)S(1)}, u32[]{:S(2)}, u32[]{:S(2)}) collective-permute-start(bf16[128,2560]{1,0:T(8,128)(2,1)S(1)} %add_convert_fusion), channel_id=1, source_target_pairs={{0,32},{1,33},{2,34},{3,35},{4,100},{5,101},{6,102},{7,103},{8,40}... | collective-permute-start | bytes 1966088 | tf_op jit(solution)/shard_map/ppermute | solution.py:49
  131.2 8.4 %collective-permute-start.22 = (bf16[64,2560]{1,0:T(8,128)(2,1)S(1)}, bf16[64,2560]{1,0:T(8,128)(2,1)S(1)}, u32[]{:S(2)}, u32[]{:S(2)}) collective-permute-start(bf16[64,2560]{1,0:T(8,128)(2,1)S(1)} %slice.138), channel_id=1, source_target_pairs={{0,96},{1,97},{2,98},{3,99},{4,36},{5,37},{6,38},{7,39},{8,104},{9... | collective-permute-start | bytes 983048 | tf_op jit(solution)/shard_map/ppermute | solution.py:49
  132.5 8.6 %collective-permute-start.27 = (bf16[64,2560]{1,0:T(8,128)(2,1)S(1)}, bf16[64,2560]{1,0:T(8,128)(2,1)S(1)}, u32[]{:S(2)}, u32[]{:S(2)}) collective-permute-start(bf16[64,2560]{1,0:T(8,128)(2,1)S(1)} %slice.137), channel_id=1, source_target_pairs={{0,3},{1,2},{2,1},{3,0},{4,5},{5,4},{6,7},{7,6},{8,11},{9,10},{10,... | collective-permute-start | bytes 983048 | tf_op jit(solution)/shard_map/ppermute | solution.py:49
  139.6 5.4 %collective-permute-start.23 = (bf16[32,2560]{1,0:T(8,128)(2,1)S(1)}, bf16[32,2560]{1,0:T(8,128)(2,1)S(1)}, u32[]{:S(2)}, u32[]{:S(2)}) collective-permute-start(bf16[32,2560]{1,0:T(8,128)(2,1)S(1)} %slice.141), channel_id=1, source_target_pairs={{0,1},{1,0},{2,3},{3,2},{4,7},{5,6},{6,5},{7,4},{8,9},{9,8},{10,11... | collective-permute-start | bytes 491528 | tf_op jit(solution)/shard_map/ppermute | solution.py:49
  141.2 6.9 %collective-permute-start.28 = (bf16[32,2560]{1,0:T(8,128)(2,1)S(1)}, bf16[32,2560]{1,0:T(8,128)(2,1)S(1)}, u32[]{:S(2)}, u32[]{:S(2)}) collective-permute-start(bf16[32,2560]{1,0:T(8,128)(2,1)S(1)} %slice.140), channel_id=1, source_target_pairs={{0,96},{1,97},{2,98},{3,99},{4,36},{5,37},{6,38},{7,39},{8,104},{9... | collective-permute-start | bytes 491528 | tf_op jit(solution)/shard_map/ppermute | solution.py:49
where the time goes:
time: 150 us; the launch traced here: 149 us
  waiting for transfers between devices  69.3 us (46%)
  starting transfers between devices  40.8 us (27%)
  Pallas kernels  21.2 us (14%)
  matrix products  7.36 us (5%)
  other arithmetic  5.74 us (4%)
  local copies, waits for them, and re-layouts  3.32 us (2%)
    ppermute x29, waiting for transfers between devices, send(): return lax.ppermute(values, AXES, pairs(flip_core0, flip_core1))  69.3 us
    ppermute x29, starting transfers between devices, send(): return lax.ppermute(values, AXES, pairs(flip_core0, flip_core1))  40.8 us
    pallas_call x1, Pallas kernels, feed_forward_first(): pl.pallas_call(kernel, out_shape=shapes, in_specs=[WHOLE] * (count + part...  8.38 us
    pallas_call x2, Pallas kernels, feed_forward(): pl.pallas_call(kernel, out_shape=[jax.ShapeDtypeStruct(p.shape, t) for p,...  7.42 us
    dot_general x1, matrix products, per_device(): jnp.einsum('sd,dkc->ksc', normed, qkv_weight, preferred_element_type=f32)  5.63 us
    pallas_call x1, Pallas kernels, attention(): pl.pallas_call(kernel, out_shape=[jax.ShapeDtypeStruct((slots, local_kv *...  5.45 us
    reduce_sum x2, other arithmetic, rms_scale(): mean_sq = jnp.mean(values * values, axis=-1, keepdims=True)  3.25 us
  transfers between devices with their start and end apart: 29, of which 14 were waited for; matrix products, arithmetic and copies ran while one was open for 4% of the time, Pallas kernels for 11%

commit v1 on v0

--- a/solution.py
+++ b/solution.py
@@ -157,12 +157,14 @@
     gate, upper = hidden[:, :units], hidden[:, units:]
     act = (gate / (1.0 + jnp.exp(-gate)) * upper).astype(bf16)
     out = jnp.dot(act, down_ref[...], preferred_element_type=f32)
+    starts = starts_of(outs)
     for i, piece in enumerate(outs):
         piece[...] = out[starts[i] : starts[i + 1], :].astype(piece.dtype)
 
 
-def feed_forward(pieces, gate_upper, down, out_types):
+def feed_forward(pieces, gate_upper, down, outs):
     count = len(pieces)
+    width = down.shape[1]
 
     def kernel(*refs):
         feed_forward_body(
@@ -171,10 +173,10 @@
 
     return pl.pallas_call(
         kernel,
-        out_shape=[jax.ShapeDtypeStruct(p.shape, t) for p, t in zip(pieces, out_types)],
+        out_shape=[jax.ShapeDtypeStruct((r, width), t) for r, t in outs],
         in_specs=[WHOLE] * (count + 2),
-        out_specs=[WHOLE] * count,
-        scratch_shapes=[pltpu.VMEM((starts_of(pieces)[-1], down.shape[1]), bf16)],
+        out_specs=[WHOLE] * len(outs),
+        scratch_shapes=[pltpu.VMEM((starts_of(pieces)[-1], width), bf16)],
         compiler_params=pltpu.CompilerParams(vmem_limit_bytes=VMEM_LIMIT),
         interpret=INTERPRET,
     )(*pieces, gate_upper, down)
@@ -242,7 +244,9 @@
     own2 = send(own, "xb", "xa")
     own3 = send(own1, "xb", "xa")
     chip_half = [own, own1, own2, own3]
-    shards = chip_half + [send(w, "core", "core") for w in chip_half]
+    shards = list(chip_half)
+    for held in chip_half:
+        shards.append(send(held, "core", "core"))
 
     first = jnp.where(core == 0, 1, 3)
     second = jnp.where(core == 0, 3, 1)
@@ -278,23 +282,26 @@
             came = cube_send(jnp.concatenate([even[i], odd[i]]), i, step)
             even[i] = jnp.concatenate([even[i], came[:count]])
             odd[i] = jnp.concatenate([odd[i], came[count:]])
-    far_odd, far_even = [], []
+    far = []
     for i in range(2):
-        far_odd.append(cube_send(odd[i], i, 3))
-    for i in range(2):
-        far_even.append(cube_send(even[i], i, 3))
+        far.append(cube_send(jnp.concatenate([odd[i], even[i]]), i, 3))
 
     outs, gate_upper, down = feed_forward_first(odd + even, shards, (bf16, bf16, f32, f32))
     *odd_out, even0, even1 = outs
     even_out = [even0, even1]
-    far_odd_out = feed_forward(far_odd, gate_upper, down, (bf16, bf16))
-    far_even_out = feed_forward(far_even, gate_upper, down, (f32, f32))
+    far_odd_out, far_even_out = [], []
+    for i in range(2):
+        count = far[i].shape[0] // 2
+        ins, outs = (far[i],), ((count, bf16), (count, f32))
+        odd_part, even_part = feed_forward(ins, gate_upper, down, outs)
+        far_odd_out.append(odd_part)
+        far_even_out.append(even_part)
 
     total = []
     for i in range(2):
         near = even_out[i] + cube_send(odd_out[i], i, 0).astype(f32)
-        far = far_even_out[i] + cube_send(far_odd_out[i], i, 0).astype(f32)
-        total.append(near + cube_send(far.astype(bf16), i, 3).astype(f32))
+        across = far_even_out[i] + cube_send(far_odd_out[i], i, 0).astype(f32)
+        total.append(near + cube_send(across.astype(bf16), i, 3).astype(f32))
     for step in (2, 1):
         for i in range(2):
             rows = total[i].shape[0] // 2

time: 150 us -> 164 us (1.093)
  waiting for transfers between devices: 69.3 us -> 80 us
  starting transfers between devices: 40.8 us -> 45.9 us
    ppermute x29 -> x27, waiting for transfers between devices: 69.3 us -> 80 us  [send(): return lax.ppermute(values, AXES, pairs(flip_core0, flip_core1))]
    ppermute x29 -> x27, starting transfers between devices: 40.8 us -> 45.9 us  [send(): return lax.ppermute(values, AXES, pairs(flip_core0, flip_core1))]
  transfers between devices with their start and end apart: 29 -> 27, of which waited for: 14 -> 16; matrix products, arithmetic and copies ran while one was open for 4% -> 3% of each run, Pallas kernels for 11% -> 9%
where the time goes in v1:
time: 164 us
  waiting for transfers between devices  80 us (49%)
  starting transfers between devices  45.9 us (28%)
  Pallas kernels  20 us (12%)
  matrix products  7.37 us (4%)
  other arithmetic  5.44 us (3%)
  local copies, waits for them, and re-layouts  4.19 us (3%)
    ppermute x27, waiting for transfers between devices, send(): return lax.ppermute(values, AXES, pairs(flip_core0, flip_core1))  80 us
    ppermute x27, starting transfers between devices, send(): return lax.ppermute(values, AXES, pairs(flip_core0, flip_core1))  45.9 us
    pallas_call x2, Pallas kernels, feed_forward(): pl.pallas_call(kernel, out_shape=[jax.ShapeDtypeStruct((r, width), t) for...  7.41 us
    pallas_call x1, Pallas kernels, feed_forward_first(): pl.pallas_call(kernel, out_shape=shapes, in_specs=[WHOLE] * (count + part...  7.11 us
    dot_general x1, matrix products, per_device(): jnp.einsum('sd,dkc->ksc', normed, qkv_weight, preferred_element_type=f32)  5.63 us
    pallas_call x1, Pallas kernels, attention(): pl.pallas_call(kernel, out_shape=[jax.ShapeDtypeStruct((slots, local_kv *...  5.45 us
  transfers between devices with their start and end apart: 27, of which 16 were waited for; matrix products, arithmetic and copies ran while one was open for 3% of the time, Pallas kernels for 9%

profile of v1, /device:TPU:0, one launch (start us, length us, event | category | flops | bytes accessed | tf_op | source)
XLA Modules:
  0.0 164.1 jit_solution(13505969593148449963)
XLA Ops:
  0.8 1.7 %fusion.2 = f32[256]{0:T(256)S(1)} fusion(bf16[256,2560]{1,0:T(8,128)(2,1)} %param.11), kind=kLoop, calls=%fused_computation.7 | loop fusion | flops 1965824 | bytes 1311744 | tf_op jit(solution)/shard_map/reduce_sum | solution.py:57
  2.7 5.6 %fusion.9.qkv_ref = f32[2,256,768]{2,1,0:T(8,128)S(1)} fusion(bf16[2560,2,768]{2,1,0:T(2,128)(2,1)} %param.15, bf16[256,2560]{1,0:T(8,128)(2,1)S(1)} %copy-done.5, f32[2560]{0:T(1024)S(1)} %copy-done.9, f32[256]{0:T(256)S(1)} %add_rsqrt_fusion), kind=kOutput, calls=%fused_computation.16 | convolution fusion | flops 2015887360 | bytes 10759168 | tf_op jit(solution)/shard_map/sd,dkc->ksc/dot_general | solution.py:254
  8.3 5.4 %shard_map.122 = (bf16[256,1024]{1,0:T(8,128)(2,1)S(1)}, bf16[2,2,256,128]{3,2,1,0:T(8,128)(2,1)S(1)}) custom-call(s32[1,4]{1,0:T(1,128)S(1)} %copy-done, s32[1,16]{1,0:T(1,128)S(1)} %copy-done.1, s32[1,3]{1,0:T(1,128)S(1)} %add_bitcast_fusion.place_ref, f32[2,256,768]{2,1,0:T(8,128)S(1)} %fusion.9.qkv_ref, f32[1,128]{1,0:T(1,128)S(1)} %bitcast.25, ...), custom_call_target="tpu_custom_call" | custom-call | tf_op jit(solution)/shard_map/pallas_call | solution.py:132
  13.8 0.9 convolution_convert_fusion
  14.7 2.1 %collective-permute-start = (bf16[128,2560]{1,0:T(8,128)(2,1)S(1)}, bf16[128,2560]{1,0:T(8,128)(2,1)S(1)}, u32[]{:S(2)}, u32[]{:S(2)}) collective-permute-start(bf16[128,2560]{1,0:T(8,128)(2,1)S(1)} %convolution_convert_fusion), channel_id=1, source_target_pairs={{0,1},{1,0},{2,3},{3,2},{4,7},{5,6},{6,5},{7,4},{8,9},{9,8},{10,11... | collective-permute-start | bytes 1966088 | tf_op jit(solution)/shard_map/ppermute | solution.py:49
  16.8 0.9 fusion.21
  17.7 1.1 fusion.24
  18.8 6.6 %collective-permute-done = bf16[128,2560]{1,0:T(8,128)(2,1)S(1)} collective-permute-done((bf16[128,2560]{1,0:T(8,128)(2,1)S(1)}, bf16[128,2560]{1,0:T(8,128)(2,1)S(1)}, u32[]{:S(2)}, u32[]{:S(2)}) %collective-permute-start) | collective-permute-done | bytes 655392 | tf_op jit(solution)/shard_map/ppermute | solution.py:49
  25.5 0.8 slice.149
  26.3 4.1 %collective-permute-start.1 = (bf16[64,2560]{1,0:T(8,128)(2,1)}, bf16[64,2560]{1,0:T(8,128)(2,1)}, u32[]{:S(2)}, u32[]{:S(2)}) collective-permute-start(bf16[64,2560]{1,0:T(8,128)(2,1)} %slice.149), channel_id=1, source_target_pairs={{0,3},{1,2},{2,1},{3,0},{4,5},{5,4},{6,7},{7,6},{8,11},{9,10},{10,... | collective-permute-start | bytes 983048 | tf_op jit(solution)/shard_map/ppermute | solution.py:49
  30.4 0.8 copy_bitcast_fusion
  31.3 4.5 %collective-permute-done.1 = bf16[64,2560]{1,0:T(8,128)(2,1)} collective-permute-done((bf16[64,2560]{1,0:T(8,128)(2,1)}, bf16[64,2560]{1,0:T(8,128)(2,1)}, u32[]{:S(2)}, u32[]{:S(2)}) %collective-permute-start.1) | collective-permute-done | bytes 327712 | tf_op jit(solution)/shard_map/ppermute | solution.py:49
  35.8 1.2 multiply_reduce_fusion
  37.2 1.7 %collective-permute-start.2 = (bf16[32,2560]{1,0:T(8,128)(2,1)S(1)}, bf16[32,2560]{1,0:T(8,128)(2,1)S(1)}, u32[]{:S(2)}, u32[]{:S(2)}) collective-permute-start(bf16[32,2560]{1,0:T(8,128)(2,1)S(1)} %get-tuple-element.41), channel_id=1, source_target_pairs={{0,32},{1,33},{2,34},{3,35},{4,100},{5,101},{6,102},{7,103},{8,40}... | collective-permute-start | bytes 491528 | tf_op jit(solution)/shard_map/ppermute | solution.py:49
  39.1 2.8 %collective-permute-start.9 = (bf16[240,2560]{1,0:T(8,128)(2,1)S(1)}, bf16[240,2560]{1,0:T(8,128)(2,1)S(1)}, u32[]{:S(2)}, u32[]{:S(2)}) collective-permute-start(bf16[240,2560]{1,0:T(8,128)(2,1)S(1)} %fusion.17.refs_4_), channel_id=1, source_target_pairs={{0,24},{1,25},{2,26},{3,27},{4,12},{5,13},{6,14},{7,15},{8,16},{9,... | collective-permute-start | bytes 3686408 | tf_op jit(solution)/shard_map/ppermute | solution.py:49
  42.1 0.5 collective-permute-done.2
  42.6 1.6 collective-permute-start.3
  44.3 3.2 %collective-permute-done.5 = bf16[32,2560]{1,0:T(8,128)(2,1)S(1)} collective-permute-done((bf16[32,2560]{1,0:T(8,128)(2,1)S(1)}, bf16[32,2560]{1,0:T(8,128)(2,1)S(1)}, u32[]{:S(2)}, u32[]{:S(2)}) %collective-permute-start.5) | collective-permute-done | bytes 163872 | tf_op jit(solution)/shard_map/ppermute | solution.py:49
  47.5 2.4 %collective-permute-start.6 = (bf16[64,2560]{1,0:T(8,128)(2,1)S(1)}, bf16[64,2560]{1,0:T(8,128)(2,1)S(1)}, u32[]{:S(2)}, u32[]{:S(2)}) collective-permute-start(bf16[64,2560]{1,0:T(8,128)(2,1)S(1)} %pad_maximum_fusion.9), channel_id=1, source_target_pairs={{0,96},{1,97},{2,98},{3,99},{4,36},{5,37},{6,38},{7,39},{8,104},{9... | collective-permute-start | bytes 983048 | tf_op jit(solution)/shard_map/ppermute | solution.py:49
  49.9 18.6 %collective-permute-done.8.refs_5_ = bf16[240,2560]{1,0:T(8,128)(2,1)S(1)} collective-permute-done((bf16[240,2560]{1,0:T(8,128)(2,1)S(1)}, bf16[240,2560]{1,0:T(8,128)(2,1)S(1)}, u32[]{:S(2)}, u32[]{:S(2)}) %collective-permute-start.8) | collective-permute-done | bytes 1228832 | tf_op jit(solution)/shard_map/ppermute | solution.py:49
  68.5 1.6 collective-permute-start.12
  70.1 3.0 %collective-permute-start.10 = (bf16[240,2560]{1,0:T(8,128)(2,1)S(1)}, bf16[240,2560]{1,0:T(8,128)(2,1)S(1)}, u32[]{:S(2)}, u32[]{:S(2)}) collective-permute-start(bf16[240,2560]{1,0:T(8,128)(2,1)S(1)} %collective-permute-done.8.refs_5_), channel_id=1, source_target_pairs={{0,24},{1,25},{2,26},{3,27},{4,12},{5,13},{6,14},{7,15},{8,16},{9,... | collective-permute-start | bytes 3686408 | tf_op jit(solution)/shard_map/ppermute | solution.py:49
  73.2 3.3 %collective-permute-start.7 = (bf16[128,2560]{1,0:T(8,128)(2,1)S(1)}, bf16[128,2560]{1,0:T(8,128)(2,1)S(1)}, u32[]{:S(2)}, u32[]{:S(2)}) collective-permute-start(bf16[128,2560]{1,0:T(8,128)(2,1)S(1)} %pad_maximum_fusion.3), channel_id=1, source_target_pairs={{0,3},{1,2},{2,1},{3,0},{4,5},{5,4},{6,7},{7,6},{8,11},{9,10},{10,... | collective-permute-start | bytes 1966088 | tf_op jit(solution)/shard_map/ppermute | solution.py:49
  76.6 8.5 %collective-permute-done.7 = bf16[128,2560]{1,0:T(8,128)(2,1)S(1)} collective-permute-done((bf16[128,2560]{1,0:T(8,128)(2,1)S(1)}, bf16[128,2560]{1,0:T(8,128)(2,1)S(1)}, u32[]{:S(2)}, u32[]{:S(2)}) %collective-permute-start.7) | collective-permute-done | bytes 655392 | tf_op jit(solution)/shard_map/ppermute | solution.py:49
  85.1 2.3 %collective-permute-start.4 = (bf16[128,2560]{1,0:T(8,128)(2,1)S(1)}, bf16[128,2560]{1,0:T(8,128)(2,1)S(1)}, u32[]{:S(2)}, u32[]{:S(2)}) collective-permute-start(bf16[128,2560]{1,0:T(8,128)(2,1)S(1)} %pad_maximum_fusion), channel_id=1, source_target_pairs={{0,96},{1,97},{2,98},{3,99},{4,36},{5,37},{6,38},{7,39},{8,104},{9... | collective-permute-start | bytes 1966088 | tf_op jit(solution)/shard_map/ppermute | solution.py:49
  87.5 9.4 %collective-permute-done.4 = bf16[128,2560]{1,0:T(8,128)(2,1)S(1)} collective-permute-done((bf16[128,2560]{1,0:T(8,128)(2,1)S(1)}, bf16[128,2560]{1,0:T(8,128)(2,1)S(1)}, u32[]{:S(2)}, u32[]{:S(2)}) %collective-permute-start.4) | collective-permute-done | bytes 655392 | tf_op jit(solution)/shard_map/ppermute | solution.py:49
  97.4 3.3 %collective-permute-start.16 = (bf16[256,2560]{1,0:T(8,128)(2,1)S(1)}, bf16[256,2560]{1,0:T(8,128)(2,1)S(1)}, u32[]{:S(2)}, u32[]{:S(2)}) collective-permute-start(bf16[256,2560]{1,0:T(8,128)(2,1)S(1)} %get-tuple-element.30), channel_id=1, source_target_pairs={{0,3},{1,2},{2,1},{3,0},{4,5},{5,4},{6,7},{7,6},{8,11},{9,10},{10,... | collective-permute-start | bytes 3932168 | tf_op jit(solution)/shard_map/ppermute | solution.py:49
  100.9 7.1 %shard_map.123 = (bf16[128,2560]{1,0:T(8,128)(2,1)S(1)}, bf16[128,2560]{1,0:T(8,128)(2,1)S(1)}, f32[128,2560]{1,0:T(8,128)S(1)}, f32[128,2560]{1,0:T(8,128)S(1)}...) custom-call(bf16[128,2560]{1,0:T(8,128)(2,1)S(1)} %get-tuple-element.46.refs_0_, ...), custom_call_target="tpu_custom_call" | custom-call | tf_op jit(solution)/shard_map/pallas_call | solution.py:203
  108.0 6.7 %collective-permute-done.22.refs_0_ = bf16[256,2560]{1,0:T(8,128)(2,1)S(1)} collective-permute-done((bf16[256,2560]{1,0:T(8,128)(2,1)S(1)}, bf16[256,2560]{1,0:T(8,128)(2,1)S(1)}, u32[]{:S(2)}, u32[]{:S(2)}) %collective-permute-start.22) | collective-permute-done | bytes 1310752 | tf_op jit(solution)/shard_map/ppermute | solution.py:49
  114.7 3.7 %shard_map.125 = (bf16[128,2560]{1,0:T(8,128)(2,1)S(1)}, f32[128,2560]{1,0:T(8,128)S(1)}) custom-call(bf16[256,2560]{1,0:T(8,128)(2,1)S(1)} %collective-permute-done.22.refs_0_, bf16[1280,2560]{1,0:T(8,128)(2,1)S(1)} %get-tuple-element.17.refs_1_, bf16[640,2560]{1,0:T(8,128)(2,1)S(1)} %get-tuple-element.18.refs_2_), custom_call_target="tpu_custom_call" | custom-call | tf_op jit(solution)/shard_map/pallas_call | solution.py:174
  118.5 1.0 copy.26
  119.5 2.0 %collective-permute-start.21 = (bf16[128,2560]{1,0:T(8,128)(2,1)S(1)}, bf16[128,2560]{1,0:T(8,128)(2,1)S(1)}, u32[]{:S(2)}, u32[]{:S(2)}) collective-permute-start(bf16[128,2560]{1,0:T(8,128)(2,1)S(1)} %get-tuple-element.22), channel_id=1, source_target_pairs={{0,1},{1,0},{2,3},{3,2},{4,7},{5,6},{6,5},{7,4},{8,9},{9,8},{10,11... | collective-permute-start | bytes 1966088 | tf_op jit(solution)/shard_map/ppermute | solution.py:49
  121.5 3.7 %shard_map.124 = (bf16[128,2560]{1,0:T(8,128)(2,1)S(1)}, f32[128,2560]{1,0:T(8,128)S(1)}) custom-call(bf16[256,2560]{1,0:T(8,128)(2,1)S(1)} %collective-permute-done.16.refs_0_, bf16[1280,2560]{1,0:T(8,128)(2,1)S(1)} %get-tuple-element.17.refs_1_, bf16[640,2560]{1,0:T(8,128)(2,1)S(1)} %get-tuple-element.18.refs_2_), custom_call_target="tpu_custom_call" | custom-call | tf_op jit(solution)/shard_map/pallas_call | solution.py:174
  125.2 2.1 %collective-permute-start.17 = (bf16[128,2560]{1,0:T(8,128)(2,1)S(1)}, bf16[128,2560]{1,0:T(8,128)(2,1)S(1)}, u32[]{:S(2)}, u32[]{:S(2)}) collective-permute-start(bf16[128,2560]{1,0:T(8,128)(2,1)S(1)} %get-tuple-element.20), channel_id=1, source_target_pairs={{0,32},{1,33},{2,34},{3,35},{4,100},{5,101},{6,102},{7,103},{8,40}... | collective-permute-start | bytes 1966088 | tf_op jit(solution)/shard_map/ppermute | solution.py:49
  127.3 1.8 %collective-permute-done.23 = bf16[128,2560]{1,0:T(8,128)(2,1)S(1)} collective-permute-done((bf16[128,2560]{1,0:T(8,128)(2,1)S(1)}, bf16[128,2560]{1,0:T(8,128)(2,1)S(1)}, u32[]{:S(2)}, u32[]{:S(2)}) %collective-permute-start.23) | collective-permute-done | bytes 655392 | tf_op jit(solution)/shard_map/ppermute | solution.py:49
  129.3 7.8 %collective-permute-done.17 = bf16[128,2560]{1,0:T(8,128)(2,1)S(1)} collective-permute-done((bf16[128,2560]{1,0:T(8,128)(2,1)S(1)}, bf16[128,2560]{1,0:T(8,128)(2,1)S(1)}, u32[]{:S(2)}, u32[]{:S(2)}) %collective-permute-start.17) | collective-permute-done | bytes 655392 | tf_op jit(solution)/shard_map/ppermute | solution.py:49
  137.2 3.3 %collective-permute-start.18 = (bf16[128,2560]{1,0:T(8,128)(2,1)S(1)}, bf16[128,2560]{1,0:T(8,128)(2,1)S(1)}, u32[]{:S(2)}, u32[]{:S(2)}) collective-permute-start(bf16[128,2560]{1,0:T(8,128)(2,1)S(1)} %add_convert_fusion.1), channel_id=1, source_target_pairs={{0,3},{1,2},{2,1},{3,0},{4,5},{5,4},{6,7},{7,6},{8,11},{9,10},{10,... | collective-permute-start | bytes 1966088 | tf_op jit(solution)/shard_map/ppermute | solution.py:49
  140.5 3.6 %collective-permute-done.24 = bf16[128,2560]{1,0:T(8,128)(2,1)S(1)} collective-permute-done((bf16[128,2560]{1,0:T(8,128)(2,1)S(1)}, bf16[128,2560]{1,0:T(8,128)(2,1)S(1)}, u32[]{:S(2)}, u32[]{:S(2)}) %collective-permute-start.24) | collective-permute-done | bytes 655392 | tf_op jit(solution)/shard_map/ppermute | solution.py:49
  144.3 3.3 %collective-permute-start.25 = (bf16[64,2560]{1,0:T(8,128)(2,1)S(1)}, bf16[64,2560]{1,0:T(8,128)(2,1)S(1)}, u32[]{:S(2)}, u32[]{:S(2)}) collective-permute-start(bf16[64,2560]{1,0:T(8,128)(2,1)S(1)} %slice.147), channel_id=1, source_target_pairs={{0,3},{1,2},{2,1},{3,0},{4,5},{5,4},{6,7},{7,6},{8,11},{9,10},{10,... | collective-permute-start | bytes 983048 | tf_op jit(solution)/shard_map/ppermute | solution.py:49
  147.6 1.4 collective-permute-done.18
  149.1 0.2 convert_add_fusion.1
  149.4 2.4 %collective-permute-start.19 = (bf16[64,2560]{1,0:T(8,128)(2,1)S(1)}, bf16[64,2560]{1,0:T(8,128)(2,1)S(1)}, u32[]{:S(2)}, u32[]{:S(2)}) collective-permute-start(bf16[64,2560]{1,0:T(8,128)(2,1)S(1)} %slice.148), channel_id=1, source_target_pairs={{0,96},{1,97},{2,98},{3,99},{4,36},{5,37},{6,38},{7,39},{8,104},{9... | collective-permute-start | bytes 983048 | tf_op jit(solution)/shard_map/ppermute | solution.py:49
  151.7 1.0 collective-permute-done.25
  152.8 2.4 %collective-permute-start.26 = (bf16[32,2560]{1,0:T(8,128)(2,1)S(1)}, bf16[32,2560]{1,0:T(8,128)(2,1)S(1)}, u32[]{:S(2)}, u32[]{:S(2)}) collective-permute-start(bf16[32,2560]{1,0:T(8,128)(2,1)S(1)} %slice.150), channel_id=1, source_target_pairs={{0,96},{1,97},{2,98},{3,99},{4,36},{5,37},{6,38},{7,39},{8,104},{9... | collective-permute-start | bytes 491528 | tf_op jit(solution)/shard_map/ppermute | solution.py:49
  155.2 2.5 %collective-permute-done.19 = bf16[64,2560]{1,0:T(8,128)(2,1)S(1)} collective-permute-done((bf16[64,2560]{1,0:T(8,128)(2,1)S(1)}, bf16[64,2560]{1,0:T(8,128)(2,1)S(1)}, u32[]{:S(2)}, u32[]{:S(2)}) %collective-permute-start.19) | collective-permute-done | bytes 327712 | tf_op jit(solution)/shard_map/ppermute | solution.py:49
  157.8 1.5 collective-permute-start.20
  159.5 3.7 %collective-permute-done.20 = bf16[32,2560]{1,0:T(8,128)(2,1)S(1)} collective-permute-done((bf16[32,2560]{1,0:T(8,128)(2,1)S(1)}, bf16[32,2560]{1,0:T(8,128)(2,1)S(1)}, u32[]{:S(2)}, u32[]{:S(2)}) %collective-permute-start.20) | collective-permute-done | bytes 163872 | tf_op jit(solution)/shard_map/ppermute | solution.py:49
  163.3 0.8 fusion.19
  (84 shorter events, 2.9 us)
Async XLA Ops:
  0.6 2.0 %copy-start.5 = (bf16[256,2560]{1,0:T(8,128)(2,1)S(1)}, bf16[256,2560]{1,0:T(8,128)(2,1)}, u32[]{:S(2)}) copy-start(bf16[256,2560]{1,0:T(8,128)(2,1)} %param.11) | copy-start | bytes 3932164
  0.6 2.0 %copy-start.9 = (f32[2560]{0:T(1024)S(1)}, f32[2560]{0:T(1024)}, u32[]{:S(2)}) copy-start(f32[2560]{0:T(1024)} %param.14) | copy-start | bytes 30724
  2.5 11.3 %slice-start = ((s8[5242880]{0:T(1024)(128)(4,1)}), s8[4194304]{0:T(1024)(128)(4,1)S(1)}, s32[]{:S(2)}) async-start(s8[5242880]{0:T(1024)(128)(4,1)} %bitcast.27), calls=%async_computation | async-start | bytes 8388608
  2.6 5.7 %copy-start = (s32[1,4]{1,0:T(1,128)S(1)}, s32[1,4]{1,0:T(1,128)}, u32[]{:S(2)}) copy-start(s32[1,4]{1,0:T(1,128)} %lengths_ref.1) | copy-start | bytes 52
  2.6 5.7 %copy-start.1 = (s32[1,16]{1,0:T(1,128)S(1)}, s32[1,16]{1,0:T(1,128)}, u32[]{:S(2)}) copy-start(s32[1,16]{1,0:T(1,128)} %pages_ref.1) | copy-start | bytes 196
  2.6 5.7 %copy-start.2 = (f32[128]{0:T(128)S(1)}, f32[128]{0:T(128)}, u32[]{:S(2)}) copy-start(f32[128]{0:T(128)} %param.16) | copy-start | bytes 1540
  2.6 5.7 %copy-start.3 = (f32[128]{0:T(128)S(1)}, f32[128]{0:T(128)}, u32[]{:S(2)}) copy-start(f32[128]{0:T(128)} %param.17) | copy-start | bytes 1540
  2.6 11.1 %slice-start.1 = ((s8[5242880]{0:T(1024)(128)(4,1)}), s8[1048576]{0:T(1024)(128)(4,1)S(1)}, s32[]{:S(2)}) async-start(s8[5242880]{0:T(1024)(128)(4,1)} %bitcast.27), calls=%async_computation.1 | async-start | bytes 2097152
  14.7 3.0 %copy-start.4 = (bf16[76,2,2560]{2,1,0:T(2,128)(2,1)S(1)}, bf16[76,2,2560]{2,1,0:T(2,128)(2,1)}, u32[]{:S(2)}) copy-start(bf16[76,2,2560]{2,1,0:T(2,128)(2,1)} %param.20) | copy-start | bytes 2334724
  14.7 10.7 %collective-permute-start = (bf16[128,2560]{1,0:T(8,128)(2,1)S(1)}, bf16[128,2560]{1,0:T(8,128)(2,1)S(1)}, u32[]{:S(2)}, u32[]{:S(2)}) collective-permute-start(bf16[128,2560]{1,0:T(8,128)(2,1)S(1)} %convolution_convert_fusion), channel_id=1, source_target_pairs={{0,1},{1,0},{2,3},{3,2},{4,7},{5,6},{6,5},{7,4},{8,9},{9,8},{10,11... | collective-permute-start | bytes 1966088 | tf_op jit(solution)/shard_map/ppermute | solution.py:49
  26.3 9.5 %collective-permute-start.1 = (bf16[64,2560]{1,0:T(8,128)(2,1)}, bf16[64,2560]{1,0:T(8,128)(2,1)}, u32[]{:S(2)}, u32[]{:S(2)}) collective-permute-start(bf16[64,2560]{1,0:T(8,128)(2,1)} %slice.149), channel_id=1, source_target_pairs={{0,3},{1,2},{2,1},{3,0},{4,5},{5,4},{6,7},{7,6},{8,11},{9,10},{10,... | collective-permute-start | bytes 983048 | tf_op jit(solution)/shard_map/ppermute | solution.py:49
  31.3 5.8 %copy-start.8 = (f32[2560]{0:T(1024)S(1)}, f32[2560]{0:T(1024)}, u32[]{:S(2)}) copy-start(f32[2560]{0:T(1024)} %param.19) | copy-start | bytes 30724
  37.0 1.9 %copy-start.6 = (bf16[76,2560]{1,0:T(8,128)(2,1)S(1)}, bf16[76,2560]{1,0:T(8,128)(2,1)}, u32[]{:S(2)}) copy-start(bf16[76,2560]{1,0:T(8,128)(2,1)} %get-tuple-element.49) | copy-start | bytes 1167364
  37.0 1.9 %copy-start.7 = (bf16[76,2560]{1,0:T(8,128)(2,1)S(1)}, bf16[76,2560]{1,0:T(8,128)(2,1)}, u32[]{:S(2)}) copy-start(bf16[76,2560]{1,0:T(8,128)(2,1)} %param.21) | copy-start | bytes 1167364
  37.2 5.4 %collective-permute-start.2 = (bf16[32,2560]{1,0:T(8,128)(2,1)S(1)}, bf16[32,2560]{1,0:T(8,128)(2,1)S(1)}, u32[]{:S(2)}, u32[]{:S(2)}) collective-permute-start(bf16[32,2560]{1,0:T(8,128)(2,1)S(1)} %get-tuple-element.41), channel_id=1, source_target_pairs={{0,32},{1,33},{2,34},{3,35},{4,100},{5,101},{6,102},{7,103},{8,40}... | collective-permute-start | bytes 491528 | tf_op jit(solution)/shard_map/ppermute | solution.py:49
  39.0 58.4 %collective-permute-start.11 = (bf16[240,2560]{1,0:T(8,128)(2,1)S(1)}, bf16[240,2560]{1,0:T(8,128)(2,1)S(1)}, u32[]{:S(2)}, u32[]{:S(2)}) collective-permute-start(bf16[240,2560]{1,0:T(8,128)(2,1)S(1)} %fusion.17.refs_4_), channel_id=1, source_target_pairs={{0,4},{1,5},{2,6},{3,7},{4,0},{5,1},{6,2},{7,3},{8,12},{9,13},{10,... | collective-permute-start | bytes 3686408 | tf_op jit(solution)/shard_map/ppermute | solution.py:49
  39.1 31.0 %collective-permute-start.9 = (bf16[240,2560]{1,0:T(8,128)(2,1)S(1)}, bf16[240,2560]{1,0:T(8,128)(2,1)S(1)}, u32[]{:S(2)}, u32[]{:S(2)}) collective-permute-start(bf16[240,2560]{1,0:T(8,128)(2,1)S(1)} %fusion.17.refs_4_), channel_id=1, source_target_pairs={{0,24},{1,25},{2,26},{3,27},{4,12},{5,13},{6,14},{7,15},{8,16},{9,... | collective-permute-start | bytes 3686408 | tf_op jit(solution)/shard_map/ppermute | solution.py:49
  41.9 26.6 %collective-permute-start.8 = (bf16[240,2560]{1,0:T(8,128)(2,1)S(1)}, bf16[240,2560]{1,0:T(8,128)(2,1)S(1)}, u32[]{:S(2)}, u32[]{:S(2)}) collective-permute-start(bf16[240,2560]{1,0:T(8,128)(2,1)S(1)} %fusion.17.refs_4_), channel_id=1, source_target_pairs={{0,8},{1,9},{2,10},{3,11},{4,28},{5,29},{6,30},{7,31},{8,0},{9,1},... | collective-permute-start | bytes 3686408 | tf_op jit(solution)/shard_map/ppermute | solution.py:49
  42.1 5.3 %collective-permute-start.5 = (bf16[32,2560]{1,0:T(8,128)(2,1)S(1)}, bf16[32,2560]{1,0:T(8,128)(2,1)S(1)}, u32[]{:S(2)}, u32[]{:S(2)}) collective-permute-start(bf16[32,2560]{1,0:T(8,128)(2,1)S(1)} %get-tuple-element.42), channel_id=1, source_target_pairs={{0,1},{1,0},{2,3},{3,2},{4,7},{5,6},{6,5},{7,4},{8,9},{9,8},{10,11... | collective-permute-start | bytes 491528 | tf_op jit(solution)/shard_map/ppermute | solution.py:49
  42.6 30.6 %collective-permute-start.3 = (bf16[64,2560]{1,0:T(8,128)(2,1)S(1)}, bf16[64,2560]{1,0:T(8,128)(2,1)S(1)}, u32[]{:S(2)}, u32[]{:S(2)}) collective-permute-start(bf16[64,2560]{1,0:T(8,128)(2,1)S(1)} %pad_maximum_fusion.8), channel_id=1, source_target_pairs={{0,1},{1,0},{2,3},{3,2},{4,7},{5,6},{6,5},{7,4},{8,9},{9,8},{10,11... | collective-permute-start | bytes 983048 | tf_op jit(solution)/shard_map/ppermute | solution.py:49
  47.5 25.7 %collective-permute-start.6 = (bf16[64,2560]{1,0:T(8,128)(2,1)S(1)}, bf16[64,2560]{1,0:T(8,128)(2,1)S(1)}, u32[]{:S(2)}, u32[]{:S(2)}) collective-permute-start(bf16[64,2560]{1,0:T(8,128)(2,1)S(1)} %pad_maximum_fusion.9), channel_id=1, source_target_pairs={{0,96},{1,97},{2,98},{3,99},{4,36},{5,37},{6,38},{7,39},{8,104},{9... | collective-permute-start | bytes 983048 | tf_op jit(solution)/shard_map/ppermute | solution.py:49
  68.5 32.4 %collective-permute-start.12 = (bf16[240,2560]{1,0:T(8,128)(2,1)S(1)}, bf16[240,2560]{1,0:T(8,128)(2,1)S(1)}, u32[]{:S(2)}, u32[]{:S(2)}) collective-permute-start(bf16[240,2560]{1,0:T(8,128)(2,1)S(1)} %collective-permute-done.8.refs_5_), channel_id=1, source_target_pairs={{0,4},{1,5},{2,6},{3,7},{4,0},{5,1},{6,2},{7,3},{8,12},{9,13},{10,... | collective-permute-start | bytes 3686408 | tf_op jit(solution)/shard_map/ppermute | solution.py:49
  70.1 27.1 %collective-permute-start.10 = (bf16[240,2560]{1,0:T(8,128)(2,1)S(1)}, bf16[240,2560]{1,0:T(8,128)(2,1)S(1)}, u32[]{:S(2)}, u32[]{:S(2)}) collective-permute-start(bf16[240,2560]{1,0:T(8,128)(2,1)S(1)} %collective-permute-done.8.refs_5_), channel_id=1, source_target_pairs={{0,24},{1,25},{2,26},{3,27},{4,12},{5,13},{6,14},{7,15},{8,16},{9,... | collective-permute-start | bytes 3686408 | tf_op jit(solution)/shard_map/ppermute | solution.py:49
  73.1 27.7 %collective-permute-start.13 = (bf16[240,2560]{1,0:T(8,128)(2,1)S(1)}, bf16[240,2560]{1,0:T(8,128)(2,1)S(1)}, u32[]{:S(2)}, u32[]{:S(2)}) collective-permute-start(bf16[240,2560]{1,0:T(8,128)(2,1)S(1)} %collective-permute-done.9.refs_6_), channel_id=1, source_target_pairs={{0,4},{1,5},{2,6},{3,7},{4,0},{5,1},{6,2},{7,3},{8,12},{9,13},{10,... | collective-permute-start | bytes 3686408 | tf_op jit(solution)/shard_map/ppermute | solution.py:49
  73.2 11.9 %collective-permute-start.7 = (bf16[128,2560]{1,0:T(8,128)(2,1)S(1)}, bf16[128,2560]{1,0:T(8,128)(2,1)S(1)}, u32[]{:S(2)}, u32[]{:S(2)}) collective-permute-start(bf16[128,2560]{1,0:T(8,128)(2,1)S(1)} %pad_maximum_fusion.3), channel_id=1, source_target_pairs={{0,3},{1,2},{2,1},{3,0},{4,5},{5,4},{6,7},{7,6},{8,11},{9,10},{10,... | collective-permute-start | bytes 1966088 | tf_op jit(solution)/shard_map/ppermute | solution.py:49
  85.1 11.8 %collective-permute-start.4 = (bf16[128,2560]{1,0:T(8,128)(2,1)S(1)}, bf16[128,2560]{1,0:T(8,128)(2,1)S(1)}, u32[]{:S(2)}, u32[]{:S(2)}) collective-permute-start(bf16[128,2560]{1,0:T(8,128)(2,1)S(1)} %pad_maximum_fusion), channel_id=1, source_target_pairs={{0,96},{1,97},{2,98},{3,99},{4,36},{5,37},{6,38},{7,39},{8,104},{9... | collective-permute-start | bytes 1966088 | tf_op jit(solution)/shard_map/ppermute | solution.py:49
  97.0 17.7 %collective-permute-start.22 = (bf16[256,2560]{1,0:T(8,128)(2,1)S(1)}, bf16[256,2560]{1,0:T(8,128)(2,1)S(1)}, u32[]{:S(2)}, u32[]{:S(2)}) collective-permute-start(bf16[256,2560]{1,0:T(8,128)(2,1)S(1)} %constant_dynamic-update-slice_fusion.6), channel_id=1, source_target_pairs={{0,32},{1,33},{2,34},{3,35},{4,100},{5,101},{6,102},{7,103},{8,40}... | collective-permute-start | bytes 3932168 | tf_op jit(solution)/shard_map/ppermute | solution.py:49
  97.1 3.7 %collective-permute-start.14 = (bf16[240,2560]{1,0:T(8,128)(2,1)S(1)}, bf16[240,2560]{1,0:T(8,128)(2,1)S(1)}, u32[]{:S(2)}, u32[]{:S(2)}) collective-permute-start(bf16[240,2560]{1,0:T(8,128)(2,1)S(1)} %collective-permute-done.10.refs_7_), channel_id=1, source_target_pairs={{0,4},{1,5},{2,6},{3,7},{4,0},{5,1},{6,2},{7,3},{8,12},{9,13},{10,... | collective-permute-start | bytes 3686408 | tf_op jit(solution)/shard_map/ppermute | solution.py:49
  97.4 24.1 %collective-permute-start.16 = (bf16[256,2560]{1,0:T(8,128)(2,1)S(1)}, bf16[256,2560]{1,0:T(8,128)(2,1)S(1)}, u32[]{:S(2)}, u32[]{:S(2)}) collective-permute-start(bf16[256,2560]{1,0:T(8,128)(2,1)S(1)} %get-tuple-element.30), channel_id=1, source_target_pairs={{0,3},{1,2},{2,1},{3,0},{4,5},{5,4},{6,7},{7,6},{8,11},{9,10},{10,... | collective-permute-start | bytes 3932168 | tf_op jit(solution)/shard_map/ppermute | solution.py:49
  118.4 10.7 %collective-permute-start.23 = (bf16[128,2560]{1,0:T(8,128)(2,1)S(1)}, bf16[128,2560]{1,0:T(8,128)(2,1)S(1)}, u32[]{:S(2)}, u32[]{:S(2)}) collective-permute-start(bf16[128,2560]{1,0:T(8,128)(2,1)S(1)} %get-tuple-element.24), channel_id=1, source_target_pairs={{0,1},{1,0},{2,3},{3,2},{4,7},{5,6},{6,5},{7,4},{8,9},{9,8},{10,11... | collective-permute-start | bytes 1966088 | tf_op jit(solution)/shard_map/ppermute | solution.py:49
  119.5 28.2 %collective-permute-start.15 = (bf16[128,2560]{1,0:T(8,128)(2,1)S(1)}, bf16[128,2560]{1,0:T(8,128)(2,1)S(1)}, u32[]{:S(2)}, u32[]{:S(2)}) collective-permute-start(bf16[128,2560]{1,0:T(8,128)(2,1)S(1)} %get-tuple-element.16), channel_id=1, source_target_pairs={{0,32},{1,33},{2,34},{3,35},{4,100},{5,101},{6,102},{7,103},{8,40}... | collective-permute-start | bytes 1966088 | tf_op jit(solution)/shard_map/ppermute | solution.py:49
  119.5 21.0 %collective-permute-start.21 = (bf16[128,2560]{1,0:T(8,128)(2,1)S(1)}, bf16[128,2560]{1,0:T(8,128)(2,1)S(1)}, u32[]{:S(2)}, u32[]{:S(2)}) collective-permute-start(bf16[128,2560]{1,0:T(8,128)(2,1)S(1)} %get-tuple-element.22), channel_id=1, source_target_pairs={{0,1},{1,0},{2,3},{3,2},{4,7},{5,6},{6,5},{7,4},{8,9},{9,8},{10,11... | collective-permute-start | bytes 1966088 | tf_op jit(solution)/shard_map/ppermute | solution.py:49
  125.2 11.9 %collective-permute-start.17 = (bf16[128,2560]{1,0:T(8,128)(2,1)S(1)}, bf16[128,2560]{1,0:T(8,128)(2,1)S(1)}, u32[]{:S(2)}, u32[]{:S(2)}) collective-permute-start(bf16[128,2560]{1,0:T(8,128)(2,1)S(1)} %get-tuple-element.20), channel_id=1, source_target_pairs={{0,32},{1,33},{2,34},{3,35},{4,100},{5,101},{6,102},{7,103},{8,40}... | collective-permute-start | bytes 1966088 | tf_op jit(solution)/shard_map/ppermute | solution.py:49
  129.2 14.9 %collective-permute-start.24 = (bf16[128,2560]{1,0:T(8,128)(2,1)S(1)}, bf16[128,2560]{1,0:T(8,128)(2,1)S(1)}, u32[]{:S(2)}, u32[]{:S(2)}) collective-permute-start(bf16[128,2560]{1,0:T(8,128)(2,1)S(1)} %add_convert_fusion), channel_id=1, source_target_pairs={{0,32},{1,33},{2,34},{3,35},{4,100},{5,101},{6,102},{7,103},{8,40}... | collective-permute-start | bytes 1966088 | tf_op jit(solution)/shard_map/ppermute | solution.py:49
  137.2 11.9 %collective-permute-start.18 = (bf16[128,2560]{1,0:T(8,128)(2,1)S(1)}, bf16[128,2560]{1,0:T(8,128)(2,1)S(1)}, u32[]{:S(2)}, u32[]{:S(2)}) collective-permute-start(bf16[128,2560]{1,0:T(8,128)(2,1)S(1)} %add_convert_fusion.1), channel_id=1, source_target_pairs={{0,3},{1,2},{2,1},{3,0},{4,5},{5,4},{6,7},{7,6},{8,11},{9,10},{10,... | collective-permute-start | bytes 1966088 | tf_op jit(solution)/shard_map/ppermute | solution.py:49
  144.3 8.4 %collective-permute-start.25 = (bf16[64,2560]{1,0:T(8,128)(2,1)S(1)}, bf16[64,2560]{1,0:T(8,128)(2,1)S(1)}, u32[]{:S(2)}, u32[]{:S(2)}) collective-permute-start(bf16[64,2560]{1,0:T(8,128)(2,1)S(1)} %slice.147), channel_id=1, source_target_pairs={{0,3},{1,2},{2,1},{3,0},{4,5},{5,4},{6,7},{7,6},{8,11},{9,10},{10,... | collective-permute-start | bytes 983048 | tf_op jit(solution)/shard_map/ppermute | solution.py:49
  149.4 8.4 %collective-permute-start.19 = (bf16[64,2560]{1,0:T(8,128)(2,1)S(1)}, bf16[64,2560]{1,0:T(8,128)(2,1)S(1)}, u32[]{:S(2)}, u32[]{:S(2)}) collective-permute-start(bf16[64,2560]{1,0:T(8,128)(2,1)S(1)} %slice.148), channel_id=1, source_target_pairs={{0,96},{1,97},{2,98},{3,99},{4,36},{5,37},{6,38},{7,39},{8,104},{9... | collective-permute-start | bytes 983048 | tf_op jit(solution)/shard_map/ppermute | solution.py:49
  152.8 6.7 %collective-permute-start.26 = (bf16[32,2560]{1,0:T(8,128)(2,1)S(1)}, bf16[32,2560]{1,0:T(8,128)(2,1)S(1)}, u32[]{:S(2)}, u32[]{:S(2)}) collective-permute-start(bf16[32,2560]{1,0:T(8,128)(2,1)S(1)} %slice.150), channel_id=1, source_target_pairs={{0,96},{1,97},{2,98},{3,99},{4,36},{5,37},{6,38},{7,39},{8,104},{9... | collective-permute-start | bytes 491528 | tf_op jit(solution)/shard_map/ppermute | solution.py:49
  157.8 5.4 %collective-permute-start.20 = (bf16[32,2560]{1,0:T(8,128)(2,1)S(1)}, bf16[32,2560]{1,0:T(8,128)(2,1)S(1)}, u32[]{:S(2)}, u32[]{:S(2)}) collective-permute-start(bf16[32,2560]{1,0:T(8,128)(2,1)S(1)} %slice.151), channel_id=1, source_target_pairs={{0,1},{1,0},{2,3},{3,2},{4,7},{5,6},{6,5},{7,4},{8,9},{9,8},{10,11... | collective-permute-start | bytes 491528 | tf_op jit(solution)/shard_map/ppermute | solution.py:49

commit v2 on v1

--- a/solution.py
+++ b/solution.py
@@ -282,20 +282,18 @@
             came = cube_send(jnp.concatenate([even[i], odd[i]]), i, step)
             even[i] = jnp.concatenate([even[i], came[:count]])
             odd[i] = jnp.concatenate([odd[i], came[count:]])
-    far = []
+    far_odd, far_even = [], []
     for i in range(2):
-        far.append(cube_send(jnp.concatenate([odd[i], even[i]]), i, 3))
+        far_odd.append(cube_send(odd[i], i, 3))
+    for i in range(2):
+        far_even.append(cube_send(even[i], i, 3))
 
     outs, gate_upper, down = feed_forward_first(odd + even, shards, (bf16, bf16, f32, f32))
     *odd_out, even0, even1 = outs
     even_out = [even0, even1]
-    far_odd_out, far_even_out = [], []
-    for i in range(2):
-        count = far[i].shape[0] // 2
-        ins, outs = (far[i],), ((count, bf16), (count, f32))
-        odd_part, even_part = feed_forward(ins, gate_upper, down, outs)
-        far_odd_out.append(odd_part)
-        far_even_out.append(even_part)
+    count = far_odd[0].shape[0]
+    far_odd_out = feed_forward(far_odd, gate_upper, down, ((count, bf16), (count, bf16)))
+    far_even_out = feed_forward(far_even, gate_upper, down, ((count, f32), (count, f32)))
 
     total = []
     for i in range(2):

time: 164 us -> 150 us (0.915)
  waiting for transfers between devices: 80 us -> 69.3 us
  starting transfers between devices: 45.9 us -> 40.8 us
    ppermute x27 -> x29, waiting for transfers between devices: 80 us -> 69.3 us  [send(): return lax.ppermute(values, AXES, pairs(flip_core0, flip_core1))]
    ppermute x27 -> x29, starting transfers between devices: 45.9 us -> 40.8 us  [send(): return lax.ppermute(values, AXES, pairs(flip_core0, flip_core1))]
  transfers between devices with their start and end apart: 27 -> 29, of which waited for: 16 -> 14; matrix products, arithmetic and copies ran while one was open for 3% -> 4% of each run, Pallas kernels for 9% -> 11%
where the time goes in v2:
time: 150 us; the launch traced here: 149 us
  waiting for transfers between devices  69.3 us (46%)
  starting transfers between devices  40.8 us (27%)
  Pallas kernels  21.2 us (14%)
  matrix products  7.36 us (5%)
  other arithmetic  5.74 us (4%)
  local copies, waits for them, and re-layouts  3.32 us (2%)
    ppermute x29, waiting for transfers between devices, send(): return lax.ppermute(values, AXES, pairs(flip_core0, flip_core1))  69.3 us
    ppermute x29, starting transfers between devices, send(): return lax.ppermute(values, AXES, pairs(flip_core0, flip_core1))  40.8 us
    pallas_call x1, Pallas kernels, feed_forward_first(): pl.pallas_call(kernel, out_shape=shapes, in_specs=[WHOLE] * (count + part...  8.38 us
    pallas_call x2, Pallas kernels, feed_forward(): pl.pallas_call(kernel, out_shape=[jax.ShapeDtypeStruct((r, width), t) for...  7.42 us
    dot_general x1, matrix products, per_device(): jnp.einsum('sd,dkc->ksc', normed, qkv_weight, preferred_element_type=f32)  5.63 us
    pallas_call x1, Pallas kernels, attention(): pl.pallas_call(kernel, out_shape=[jax.ShapeDtypeStruct((slots, local_kv *...  5.45 us
    reduce_sum x2, other arithmetic, rms_scale(): mean_sq = jnp.mean(values * values, axis=-1, keepdims=True)  3.25 us
  transfers between devices with their start and end apart: 29, of which 14 were waited for; matrix products, arithmetic and copies ran while one was open for 4% of the time, Pallas kernels for 11%

profile of v2, /device:TPU:0, one launch (start us, length us, event | category | flops | bytes accessed | tf_op | source)
XLA Modules:
  0.0 148.9 jit_solution(16646434771438827127)
XLA Ops:
  0.7 1.7 %fusion.2 = f32[256]{0:T(256)S(1)} fusion(bf16[256,2560]{1,0:T(8,128)(2,1)} %param.11), kind=kLoop, calls=%fused_computation.7 | loop fusion | flops 1965824 | bytes 1311744 | tf_op jit(solution)/shard_map/reduce_sum | solution.py:57
  2.7 5.6 %fusion.9.qkv_ref = f32[2,256,768]{2,1,0:T(8,128)S(1)} fusion(bf16[2560,2,768]{2,1,0:T(2,128)(2,1)} %param.15, bf16[256,2560]{1,0:T(8,128)(2,1)S(1)} %copy-done.6, f32[2560]{0:T(1024)S(1)} %copy-done.9, f32[256]{0:T(256)S(1)} %add_rsqrt_fusion), kind=kOutput, calls=%fused_computation.16 | convolution fusion | flops 2015887360 | bytes 10759168 | tf_op jit(solution)/shard_map/sd,dkc->ksc/dot_general | solution.py:254
  8.3 5.4 %shard_map.122 = (bf16[256,1024]{1,0:T(8,128)(2,1)S(1)}, bf16[2,2,256,128]{3,2,1,0:T(8,128)(2,1)S(1)}) custom-call(s32[1,4]{1,0:T(1,128)S(1)} %copy-done, s32[1,16]{1,0:T(1,128)S(1)} %copy-done.1, s32[1,3]{1,0:T(1,128)S(1)} %add_bitcast_fusion.place_ref, f32[2,256,768]{2,1,0:T(8,128)S(1)} %fusion.9.qkv_ref, f32[1,128]{1,0:T(1,128)S(1)} %bitcast.25, ...), custom_call_target="tpu_custom_call" | custom-call | tf_op jit(solution)/shard_map/pallas_call | solution.py:132
  13.8 0.9 convolution_convert_fusion
  14.7 2.1 %collective-permute-start = (bf16[128,2560]{1,0:T(8,128)(2,1)S(1)}, bf16[128,2560]{1,0:T(8,128)(2,1)S(1)}, u32[]{:S(2)}, u32[]{:S(2)}) collective-permute-start(bf16[128,2560]{1,0:T(8,128)(2,1)S(1)} %convolution_convert_fusion), channel_id=1, source_target_pairs={{0,1},{1,0},{2,3},{3,2},{4,7},{5,6},{6,5},{7,4},{8,9},{9,8},{10,11... | collective-permute-start | bytes 1966088 | tf_op jit(solution)/shard_map/ppermute | solution.py:49
  16.8 0.9 fusion.21
  17.7 1.1 fusion.24
  18.9 6.5 %collective-permute-done = bf16[128,2560]{1,0:T(8,128)(2,1)S(1)} collective-permute-done((bf16[128,2560]{1,0:T(8,128)(2,1)S(1)}, bf16[128,2560]{1,0:T(8,128)(2,1)S(1)}, u32[]{:S(2)}, u32[]{:S(2)}) %collective-permute-start) | collective-permute-done | bytes 655392 | tf_op jit(solution)/shard_map/ppermute | solution.py:49
  25.6 0.8 slice.139
  26.4 4.1 %collective-permute-start.1 = (bf16[64,2560]{1,0:T(8,128)(2,1)}, bf16[64,2560]{1,0:T(8,128)(2,1)}, u32[]{:S(2)}, u32[]{:S(2)}) collective-permute-start(bf16[64,2560]{1,0:T(8,128)(2,1)} %slice.139), channel_id=1, source_target_pairs={{0,3},{1,2},{2,1},{3,0},{4,5},{5,4},{6,7},{7,6},{8,11},{9,10},{10,... | collective-permute-start | bytes 983048 | tf_op jit(solution)/shard_map/ppermute | solution.py:49
  30.6 1.6 %collective-permute-start.8 = (bf16[240,2560]{1,0:T(8,128)(2,1)S(1)}, bf16[240,2560]{1,0:T(8,128)(2,1)S(1)}, u32[]{:S(2)}, u32[]{:S(2)}) collective-permute-start(bf16[240,2560]{1,0:T(8,128)(2,1)S(1)} %fusion.17.refs_4_), channel_id=1, source_target_pairs={{0,8},{1,9},{2,10},{3,11},{4,28},{5,29},{6,30},{7,31},{8,0},{9,1},... | collective-permute-start | bytes 3686408 | tf_op jit(solution)/shard_map/ppermute | solution.py:49
  32.2 2.1 %collective-permute-start.9 = (bf16[240,2560]{1,0:T(8,128)(2,1)S(1)}, bf16[240,2560]{1,0:T(8,128)(2,1)}, u32[]{:S(2)}, u32[]{:S(2)}) collective-permute-start(bf16[240,2560]{1,0:T(8,128)(2,1)S(1)} %fusion.17.refs_4_), channel_id=1, source_target_pairs={{0,24},{1,25},{2,26},{3,27},{4,12},{5,13},{6,14},{7,15},{8,16},{9,... | collective-permute-start | bytes 3686408 | tf_op jit(solution)/shard_map/ppermute | solution.py:49
  34.3 1.6 %collective-permute-done.1 = bf16[64,2560]{1,0:T(8,128)(2,1)} collective-permute-done((bf16[64,2560]{1,0:T(8,128)(2,1)}, bf16[64,2560]{1,0:T(8,128)(2,1)}, u32[]{:S(2)}, u32[]{:S(2)}) %collective-permute-start.1) | collective-permute-done | bytes 327712 | tf_op jit(solution)/shard_map/ppermute | solution.py:49
  35.9 1.5 %multiply_reduce_fusion = (f32[64]{0:T(128)S(1)}, f32[64,2560]{1,0:T(8,128)S(1)}) fusion(bf16[64,2560]{1,0:T(8,128)(2,1)} %collective-permute-done.1, f32[128,2560]{1,0:T(8,128)} %copy-done.4, bf16[256,2560]{1,0:T(8,128)(2,1)} %param.11, s32[]{:T(128)S(6)} %select_n.17), kind=kLoop, calls=%fused_computation.45 | loop fusion | flops 982976 | bytes 1966340 | tf_op jit(solution)/shard_map/reduce_sum | solution.py:57
  37.7 0.8 collective-permute-start.11
  38.4 1.6 %collective-permute-start.2 = (bf16[32,2560]{1,0:T(8,128)(2,1)S(1)}, bf16[32,2560]{1,0:T(8,128)(2,1)S(1)}, u32[]{:S(2)}, u32[]{:S(2)}) collective-permute-start(bf16[32,2560]{1,0:T(8,128)(2,1)S(1)} %get-tuple-element.37), channel_id=1, source_target_pairs={{0,32},{1,33},{2,34},{3,35},{4,100},{5,101},{6,102},{7,103},{8,40}... | collective-permute-start | bytes 491528 | tf_op jit(solution)/shard_map/ppermute | solution.py:49
  40.0 3.0 %collective-permute-done.5 = bf16[32,2560]{1,0:T(8,128)(2,1)S(1)} collective-permute-done((bf16[32,2560]{1,0:T(8,128)(2,1)S(1)}, bf16[32,2560]{1,0:T(8,128)(2,1)S(1)}, u32[]{:S(2)}, u32[]{:S(2)}) %collective-permute-start.5) | collective-permute-done | bytes 163872 | tf_op jit(solution)/shard_map/ppermute | solution.py:49
  43.0 3.1 %collective-permute-start.6 = (bf16[64,2560]{1,0:T(8,128)(2,1)S(1)}, bf16[64,2560]{1,0:T(8,128)(2,1)S(1)}, u32[]{:S(2)}, u32[]{:S(2)}) collective-permute-start(bf16[64,2560]{1,0:T(8,128)(2,1)S(1)} %pad_maximum_fusion.9), channel_id=1, source_target_pairs={{0,96},{1,97},{2,98},{3,99},{4,36},{5,37},{6,38},{7,39},{8,104},{9... | collective-permute-start | bytes 983048 | tf_op jit(solution)/shard_map/ppermute | solution.py:49
  46.2 14.4 %collective-permute-done.8.refs_5_ = bf16[240,2560]{1,0:T(8,128)(2,1)S(1)} collective-permute-done((bf16[240,2560]{1,0:T(8,128)(2,1)S(1)}, bf16[240,2560]{1,0:T(8,128)(2,1)S(1)}, u32[]{:S(2)}, u32[]{:S(2)}) %collective-permute-start.8) | collective-permute-done | bytes 1228832 | tf_op jit(solution)/shard_map/ppermute | solution.py:49
  60.6 0.5 collective-permute-start.13
  61.2 2.3 %collective-permute-start.7 = (bf16[128,2560]{1,0:T(8,128)(2,1)S(1)}, bf16[128,2560]{1,0:T(8,128)(2,1)S(1)}, u32[]{:S(2)}, u32[]{:S(2)}) collective-permute-start(bf16[128,2560]{1,0:T(8,128)(2,1)S(1)} %pad_maximum_fusion.3), channel_id=1, source_target_pairs={{0,3},{1,2},{2,1},{3,0},{4,5},{5,4},{6,7},{7,6},{8,11},{9,10},{10,... | collective-permute-start | bytes 1966088 | tf_op jit(solution)/shard_map/ppermute | solution.py:49
  63.6 9.5 %collective-permute-done.7 = bf16[128,2560]{1,0:T(8,128)(2,1)S(1)} collective-permute-done((bf16[128,2560]{1,0:T(8,128)(2,1)S(1)}, bf16[128,2560]{1,0:T(8,128)(2,1)S(1)}, u32[]{:S(2)}, u32[]{:S(2)}) %collective-permute-start.7) | collective-permute-done | bytes 655392 | tf_op jit(solution)/shard_map/ppermute | solution.py:49
  73.1 3.0 %collective-permute-start.4 = (bf16[128,2560]{1,0:T(8,128)(2,1)S(1)}, bf16[128,2560]{1,0:T(8,128)(2,1)S(1)}, u32[]{:S(2)}, u32[]{:S(2)}) collective-permute-start(bf16[128,2560]{1,0:T(8,128)(2,1)S(1)} %pad_maximum_fusion), channel_id=1, source_target_pairs={{0,96},{1,97},{2,98},{3,99},{4,36},{5,37},{6,38},{7,39},{8,104},{9... | collective-permute-start | bytes 1966088 | tf_op jit(solution)/shard_map/ppermute | solution.py:49
  76.2 8.9 %collective-permute-done.4 = bf16[128,2560]{1,0:T(8,128)(2,1)S(1)} collective-permute-done((bf16[128,2560]{1,0:T(8,128)(2,1)S(1)}, bf16[128,2560]{1,0:T(8,128)(2,1)S(1)}, u32[]{:S(2)}, u32[]{:S(2)}) %collective-permute-start.4) | collective-permute-done | bytes 655392 | tf_op jit(solution)/shard_map/ppermute | solution.py:49
  85.1 0.4 collective-permute-start.19
  85.6 2.3 %collective-permute-start.18 = (bf16[128,2560]{1,0:T(8,128)(2,1)S(1)}, bf16[128,2560]{1,0:T(8,128)(2,1)S(1)}, u32[]{:S(2)}, u32[]{:S(2)}) collective-permute-start(bf16[128,2560]{1,0:T(8,128)(2,1)S(1)} %pad_maximum_fusion.2.refs_0_), channel_id=1, source_target_pairs={{0,3},{1,2},{2,1},{3,0},{4,5},{5,4},{6,7},{7,6},{8,11},{9,10},{10,... | collective-permute-start | bytes 1966088 | tf_op jit(solution)/shard_map/ppermute | solution.py:49
  88.1 1.7 %collective-permute-start.17 = (bf16[128,2560]{1,0:T(8,128)(2,1)S(1)}, bf16[128,2560]{1,0:T(8,128)(2,1)S(1)}, u32[]{:S(2)}, u32[]{:S(2)}) collective-permute-start(bf16[128,2560]{1,0:T(8,128)(2,1)S(1)} %pad_maximum_fusion.7.refs_3_), channel_id=1, source_target_pairs={{0,32},{1,33},{2,34},{3,35},{4,100},{5,101},{6,102},{7,103},{8,40}... | collective-permute-start | bytes 1966088 | tf_op jit(solution)/shard_map/ppermute | solution.py:49
  89.7 1.0 collective-permute-start.16
  90.7 8.4 %shard_map.123 = (bf16[128,2560]{1,0:T(8,128)(2,1)S(1)}, bf16[128,2560]{1,0:T(8,128)(2,1)S(1)}, f32[128,2560]{1,0:T(8,128)S(1)}, f32[128,2560]{1,0:T(8,128)S(1)}...) custom-call(bf16[128,2560]{1,0:T(8,128)(2,1)S(1)} %pad_maximum_fusion.2.refs_0_, ...), custom_call_target="tpu_custom_call" | custom-call | tf_op jit(solution)/shard_map/pallas_call | solution.py:203
  99.1 3.7 %shard_map.125 = (bf16[128,2560]{1,0:T(8,128)(2,1)S(1)}, bf16[128,2560]{1,0:T(8,128)(2,1)S(1)}) custom-call(bf16[128,2560]{1,0:T(8,128)(2,1)S(1)} %collective-permute-done.18.refs_0_, bf16[128,2560]{1,0:T(8,128)(2,1)S(1)} %collective-permute-done.19.refs_1_, bf16[1280,2560]{1,0:T(8,128)(2,1)S(1)} %get-tuple-element.17.refs_2_, ...), custom_call_target="tpu_custom_call" | custom-call | tf_op jit(solution)/shard_map/pallas_call | solution.py:174
  102.8 0.5 collective-permute-start.20
  103.3 1.0 copy.26
  104.3 1.6 %collective-permute-start.15 = (bf16[128,2560]{1,0:T(8,128)(2,1)S(1)}, bf16[128,2560]{1,0:T(8,128)(2,1)S(1)}, u32[]{:S(2)}, u32[]{:S(2)}) collective-permute-start(bf16[128,2560]{1,0:T(8,128)(2,1)S(1)} %get-tuple-element.16), channel_id=1, source_target_pairs={{0,32},{1,33},{2,34},{3,35},{4,100},{5,101},{6,102},{7,103},{8,40}... | collective-permute-start | bytes 1966088 | tf_op jit(solution)/shard_map/ppermute | solution.py:49
  105.9 2.0 %collective-permute-start.24 = (bf16[128,2560]{1,0:T(8,128)(2,1)S(1)}, bf16[128,2560]{1,0:T(8,128)(2,1)S(1)}, u32[]{:S(2)}, u32[]{:S(2)}) collective-permute-start(bf16[128,2560]{1,0:T(8,128)(2,1)S(1)} %get-tuple-element.22), channel_id=1, source_target_pairs={{0,1},{1,0},{2,3},{3,2},{4,7},{5,6},{6,5},{7,4},{8,9},{9,8},{10,11... | collective-permute-start | bytes 1966088 | tf_op jit(solution)/shard_map/ppermute | solution.py:49
  108.0 3.7 %shard_map.124 = (f32[128,2560]{1,0:T(8,128)S(1)}, f32[128,2560]{1,0:T(8,128)S(1)}) custom-call(bf16[128,2560]{1,0:T(8,128)(2,1)S(1)} %collective-permute-done.16.refs_0_, bf16[128,2560]{1,0:T(8,128)(2,1)S(1)} %collective-permute-done.17.refs_1_, bf16[1280,2560]{1,0:T(8,128)(2,1)S(1)} %get-tuple-element.17.refs_2_, ...), custom_call_target="tpu_custom_call" | custom-call | tf_op jit(solution)/shard_map/pallas_call | solution.py:174
  111.7 1.8 %collective-permute-done.20 = bf16[128,2560]{1,0:T(8,128)(2,1)S(1)} collective-permute-done((bf16[128,2560]{1,0:T(8,128)(2,1)S(1)}, bf16[128,2560]{1,0:T(8,128)(2,1)S(1)}, u32[]{:S(2)}, u32[]{:S(2)}) %collective-permute-start.20) | collective-permute-done | bytes 655392 | tf_op jit(solution)/shard_map/ppermute | solution.py:49
  113.7 2.3 %collective-permute-start.21 = (bf16[128,2560]{1,0:T(8,128)(2,1)S(1)}, bf16[128,2560]{1,0:T(8,128)(2,1)S(1)}, u32[]{:S(2)}, u32[]{:S(2)}) collective-permute-start(bf16[128,2560]{1,0:T(8,128)(2,1)S(1)} %add_convert_fusion.1), channel_id=1, source_target_pairs={{0,3},{1,2},{2,1},{3,0},{4,5},{5,4},{6,7},{7,6},{8,11},{9,10},{10,... | collective-permute-start | bytes 1966088 | tf_op jit(solution)/shard_map/ppermute | solution.py:49
  116.0 1.1 collective-permute-done.25
  117.2 0.4 collective-permute-start.26
  117.6 2.9 %collective-permute-done.15 = bf16[128,2560]{1,0:T(8,128)(2,1)S(1)} collective-permute-done((bf16[128,2560]{1,0:T(8,128)(2,1)S(1)}, bf16[128,2560]{1,0:T(8,128)(2,1)S(1)}, u32[]{:S(2)}, u32[]{:S(2)}) %collective-permute-start.15) | collective-permute-done | bytes 655392 | tf_op jit(solution)/shard_map/ppermute | solution.py:49
  120.5 10.4 %collective-permute-done.21 = bf16[128,2560]{1,0:T(8,128)(2,1)S(1)} collective-permute-done((bf16[128,2560]{1,0:T(8,128)(2,1)S(1)}, bf16[128,2560]{1,0:T(8,128)(2,1)S(1)}, u32[]{:S(2)}, u32[]{:S(2)}) %collective-permute-start.21) | collective-permute-done | bytes 655392 | tf_op jit(solution)/shard_map/ppermute | solution.py:49
  131.2 1.0 collective-permute-start.22
  132.5 2.3 %collective-permute-start.27 = (bf16[64,2560]{1,0:T(8,128)(2,1)S(1)}, bf16[64,2560]{1,0:T(8,128)(2,1)S(1)}, u32[]{:S(2)}, u32[]{:S(2)}) collective-permute-start(bf16[64,2560]{1,0:T(8,128)(2,1)S(1)} %slice.137), channel_id=1, source_target_pairs={{0,3},{1,2},{2,1},{3,0},{4,5},{5,4},{6,7},{7,6},{8,11},{9,10},{10,... | collective-permute-start | bytes 983048 | tf_op jit(solution)/shard_map/ppermute | solution.py:49
  134.8 4.7 %collective-permute-done.22 = bf16[64,2560]{1,0:T(8,128)(2,1)S(1)} collective-permute-done((bf16[64,2560]{1,0:T(8,128)(2,1)S(1)}, bf16[64,2560]{1,0:T(8,128)(2,1)S(1)}, u32[]{:S(2)}, u32[]{:S(2)}) %collective-permute-start.22) | collective-permute-done | bytes 327712 | tf_op jit(solution)/shard_map/ppermute | solution.py:49
  139.7 1.3 collective-permute-done.27
  141.2 3.6 %collective-permute-start.28 = (bf16[32,2560]{1,0:T(8,128)(2,1)S(1)}, bf16[32,2560]{1,0:T(8,128)(2,1)S(1)}, u32[]{:S(2)}, u32[]{:S(2)}) collective-permute-start(bf16[32,2560]{1,0:T(8,128)(2,1)S(1)} %slice.140), channel_id=1, source_target_pairs={{0,96},{1,97},{2,98},{3,99},{4,36},{5,37},{6,38},{7,39},{8,104},{9... | collective-permute-start | bytes 491528 | tf_op jit(solution)/shard_map/ppermute | solution.py:49
  145.1 3.0 %collective-permute-done.28 = bf16[32,2560]{1,0:T(8,128)(2,1)S(1)} collective-permute-done((bf16[32,2560]{1,0:T(8,128)(2,1)S(1)}, bf16[32,2560]{1,0:T(8,128)(2,1)S(1)}, u32[]{:S(2)}, u32[]{:S(2)}) %collective-permute-start.28) | collective-permute-done | bytes 163872 | tf_op jit(solution)/shard_map/ppermute | solution.py:49
  148.1 0.8 fusion.19
  (82 shorter events, 2.7 us)
Async XLA Ops:
  0.6 2.0 %copy-start.6 = (bf16[256,2560]{1,0:T(8,128)(2,1)S(1)}, bf16[256,2560]{1,0:T(8,128)(2,1)}, u32[]{:S(2)}) copy-start(bf16[256,2560]{1,0:T(8,128)(2,1)} %param.11) | copy-start | bytes 3932164
  0.6 2.0 %copy-start.9 = (f32[2560]{0:T(1024)S(1)}, f32[2560]{0:T(1024)}, u32[]{:S(2)}) copy-start(f32[2560]{0:T(1024)} %param.14) | copy-start | bytes 30724
  2.5 11.3 %slice-start = ((s8[5242880]{0:T(1024)(128)(4,1)}), s8[4194304]{0:T(1024)(128)(4,1)S(1)}, s32[]{:S(2)}) async-start(s8[5242880]{0:T(1024)(128)(4,1)} %bitcast.27), calls=%async_computation | async-start | bytes 8388608
  2.6 5.7 %copy-start = (s32[1,4]{1,0:T(1,128)S(1)}, s32[1,4]{1,0:T(1,128)}, u32[]{:S(2)}) copy-start(s32[1,4]{1,0:T(1,128)} %lengths_ref.1) | copy-start | bytes 52
  2.6 5.7 %copy-start.1 = (s32[1,16]{1,0:T(1,128)S(1)}, s32[1,16]{1,0:T(1,128)}, u32[]{:S(2)}) copy-start(s32[1,16]{1,0:T(1,128)} %pages_ref.1) | copy-start | bytes 196
  2.6 5.7 %copy-start.2 = (f32[128]{0:T(128)S(1)}, f32[128]{0:T(128)}, u32[]{:S(2)}) copy-start(f32[128]{0:T(128)} %param.16) | copy-start | bytes 1540
  2.6 5.7 %copy-start.3 = (f32[128]{0:T(128)S(1)}, f32[128]{0:T(128)}, u32[]{:S(2)}) copy-start(f32[128]{0:T(128)} %param.17) | copy-start | bytes 1540
  2.6 11.1 %slice-start.1 = ((s8[5242880]{0:T(1024)(128)(4,1)}), s8[1048576]{0:T(1024)(128)(4,1)S(1)}, s32[]{:S(2)}) async-start(s8[5242880]{0:T(1024)(128)(4,1)} %bitcast.27), calls=%async_computation.1 | async-start | bytes 2097152
  14.7 3.0 %copy-start.5 = (bf16[76,2,2560]{2,1,0:T(2,128)(2,1)S(1)}, bf16[76,2,2560]{2,1,0:T(2,128)(2,1)}, u32[]{:S(2)}) copy-start(bf16[76,2,2560]{2,1,0:T(2,128)(2,1)} %param.20) | copy-start | bytes 2334724
  14.7 10.7 %collective-permute-start = (bf16[128,2560]{1,0:T(8,128)(2,1)S(1)}, bf16[128,2560]{1,0:T(8,128)(2,1)S(1)}, u32[]{:S(2)}, u32[]{:S(2)}) collective-permute-start(bf16[128,2560]{1,0:T(8,128)(2,1)S(1)} %convolution_convert_fusion), channel_id=1, source_target_pairs={{0,1},{1,0},{2,3},{3,2},{4,7},{5,6},{6,5},{7,4},{8,9},{9,8},{10,11... | collective-permute-start | bytes 1966088 | tf_op jit(solution)/shard_map/ppermute | solution.py:49
  18.9 11.6 %copy-start.7 = (bf16[76,2560]{1,0:T(8,128)(2,1)S(1)}, bf16[76,2560]{1,0:T(8,128)(2,1)}, u32[]{:S(2)}) copy-start(bf16[76,2560]{1,0:T(8,128)(2,1)} %param.21) | copy-start | bytes 1167364
  25.5 5.0 %copy-start.4 = (f32[128,2560]{1,0:T(8,128)}, f32[128,2560]{1,0:T(8,128)S(1)}, u32[]{:S(2)}) copy-start(f32[128,2560]{1,0:T(8,128)S(1)} %convert_add_fusion.2) | copy-start | bytes 3932164
  26.4 9.5 %collective-permute-start.1 = (bf16[64,2560]{1,0:T(8,128)(2,1)}, bf16[64,2560]{1,0:T(8,128)(2,1)}, u32[]{:S(2)}, u32[]{:S(2)}) collective-permute-start(bf16[64,2560]{1,0:T(8,128)(2,1)} %slice.139), channel_id=1, source_target_pairs={{0,3},{1,2},{2,1},{3,0},{4,5},{5,4},{6,7},{7,6},{8,11},{9,10},{10,... | collective-permute-start | bytes 983048 | tf_op jit(solution)/shard_map/ppermute | solution.py:49
  30.6 6.8 %copy-start.8 = (f32[2560]{0:T(1024)S(1)}, f32[2560]{0:T(1024)}, u32[]{:S(2)}) copy-start(f32[2560]{0:T(1024)} %param.19) | copy-start | bytes 30724
  30.6 30.0 %collective-permute-start.8 = (bf16[240,2560]{1,0:T(8,128)(2,1)S(1)}, bf16[240,2560]{1,0:T(8,128)(2,1)S(1)}, u32[]{:S(2)}, u32[]{:S(2)}) collective-permute-start(bf16[240,2560]{1,0:T(8,128)(2,1)S(1)} %fusion.17.refs_4_), channel_id=1, source_target_pairs={{0,8},{1,9},{2,10},{3,11},{4,28},{5,29},{6,30},{7,31},{8,0},{9,1},... | collective-permute-start | bytes 3686408 | tf_op jit(solution)/shard_map/ppermute | solution.py:49
  32.2 28.4 %collective-permute-start.9 = (bf16[240,2560]{1,0:T(8,128)(2,1)S(1)}, bf16[240,2560]{1,0:T(8,128)(2,1)}, u32[]{:S(2)}, u32[]{:S(2)}) collective-permute-start(bf16[240,2560]{1,0:T(8,128)(2,1)S(1)} %fusion.17.refs_4_), channel_id=1, source_target_pairs={{0,24},{1,25},{2,26},{3,27},{4,12},{5,13},{6,14},{7,15},{8,16},{9,... | collective-permute-start | bytes 3686408 | tf_op jit(solution)/shard_map/ppermute | solution.py:49
  37.6 5.4 %collective-permute-start.5 = (bf16[32,2560]{1,0:T(8,128)(2,1)S(1)}, bf16[32,2560]{1,0:T(8,128)(2,1)S(1)}, u32[]{:S(2)}, u32[]{:S(2)}) collective-permute-start(bf16[32,2560]{1,0:T(8,128)(2,1)S(1)} %get-tuple-element.36), channel_id=1, source_target_pairs={{0,1},{1,0},{2,3},{3,2},{4,7},{5,6},{6,5},{7,4},{8,9},{9,8},{10,11... | collective-permute-start | bytes 491528 | tf_op jit(solution)/shard_map/ppermute | solution.py:49
  37.7 47.9 %collective-permute-start.11 = (bf16[240,2560]{1,0:T(8,128)(2,1)S(1)}, bf16[240,2560]{1,0:T(8,128)(2,1)S(1)}, u32[]{:S(2)}, u32[]{:S(2)}) collective-permute-start(bf16[240,2560]{1,0:T(8,128)(2,1)S(1)} %fusion.17.refs_4_), channel_id=1, source_target_pairs={{0,4},{1,5},{2,6},{3,7},{4,0},{5,1},{6,2},{7,3},{8,12},{9,13},{10,... | collective-permute-start | bytes 3686408 | tf_op jit(solution)/shard_map/ppermute | solution.py:49
  38.4 7.7 %collective-permute-start.2 = (bf16[32,2560]{1,0:T(8,128)(2,1)S(1)}, bf16[32,2560]{1,0:T(8,128)(2,1)S(1)}, u32[]{:S(2)}, u32[]{:S(2)}) collective-permute-start(bf16[32,2560]{1,0:T(8,128)(2,1)S(1)} %get-tuple-element.37), channel_id=1, source_target_pairs={{0,32},{1,33},{2,34},{3,35},{4,100},{5,101},{6,102},{7,103},{8,40}... | collective-permute-start | bytes 491528 | tf_op jit(solution)/shard_map/ppermute | solution.py:49
  43.0 17.6 %collective-permute-start.6 = (bf16[64,2560]{1,0:T(8,128)(2,1)S(1)}, bf16[64,2560]{1,0:T(8,128)(2,1)S(1)}, u32[]{:S(2)}, u32[]{:S(2)}) collective-permute-start(bf16[64,2560]{1,0:T(8,128)(2,1)S(1)} %pad_maximum_fusion.9), channel_id=1, source_target_pairs={{0,96},{1,97},{2,98},{3,99},{4,36},{5,37},{6,38},{7,39},{8,104},{9... | collective-permute-start | bytes 983048 | tf_op jit(solution)/shard_map/ppermute | solution.py:49
  46.1 15.1 %collective-permute-start.3 = (bf16[64,2560]{1,0:T(8,128)(2,1)S(1)}, bf16[64,2560]{1,0:T(8,128)(2,1)S(1)}, u32[]{:S(2)}, u32[]{:S(2)}) collective-permute-start(bf16[64,2560]{1,0:T(8,128)(2,1)S(1)} %pad_maximum_fusion.8), channel_id=1, source_target_pairs={{0,1},{1,0},{2,3},{3,2},{4,7},{5,6},{6,5},{7,4},{8,9},{9,8},{10,11... | collective-permute-start | bytes 983048 | tf_op jit(solution)/shard_map/ppermute | solution.py:49
  60.6 24.9 %collective-permute-start.10 = (bf16[240,2560]{1,0:T(8,128)(2,1)S(1)}, bf16[240,2560]{1,0:T(8,128)(2,1)S(1)}, u32[]{:S(2)}, u32[]{:S(2)}) collective-permute-start(bf16[240,2560]{1,0:T(8,128)(2,1)S(1)} %collective-permute-done.8.refs_5_), channel_id=1, source_target_pairs={{0,24},{1,25},{2,26},{3,27},{4,12},{5,13},{6,14},{7,15},{8,16},{9,... | collective-permute-start | bytes 3686408 | tf_op jit(solution)/shard_map/ppermute | solution.py:49
  60.6 27.4 %collective-permute-start.12 = (bf16[240,2560]{1,0:T(8,128)(2,1)S(1)}, bf16[240,2560]{1,0:T(8,128)(2,1)S(1)}, u32[]{:S(2)}, u32[]{:S(2)}) collective-permute-start(bf16[240,2560]{1,0:T(8,128)(2,1)S(1)} %collective-permute-done.8.refs_5_), channel_id=1, source_target_pairs={{0,4},{1,5},{2,6},{3,7},{4,0},{5,1},{6,2},{7,3},{8,12},{9,13},{10,... | collective-permute-start | bytes 3686408 | tf_op jit(solution)/shard_map/ppermute | solution.py:49
  60.6 29.1 %collective-permute-start.13 = (bf16[240,2560]{1,0:T(8,128)(2,1)}, bf16[240,2560]{1,0:T(8,128)(2,1)S(1)}, u32[]{:S(2)}, u32[]{:S(2)}) collective-permute-start(bf16[240,2560]{1,0:T(8,128)(2,1)} %collective-permute-done.9.refs_6_), channel_id=1, source_target_pairs={{0,4},{1,5},{2,6},{3,7},{4,0},{5,1},{6,2},{7,3},{8,12},{9,13},{10,... | collective-permute-start | bytes 3686408 | tf_op jit(solution)/shard_map/ppermute | solution.py:49
  61.2 11.9 %collective-permute-start.7 = (bf16[128,2560]{1,0:T(8,128)(2,1)S(1)}, bf16[128,2560]{1,0:T(8,128)(2,1)S(1)}, u32[]{:S(2)}, u32[]{:S(2)}) collective-permute-start(bf16[128,2560]{1,0:T(8,128)(2,1)S(1)} %pad_maximum_fusion.3), channel_id=1, source_target_pairs={{0,3},{1,2},{2,1},{3,0},{4,5},{5,4},{6,7},{7,6},{8,11},{9,10},{10,... | collective-permute-start | bytes 1966088 | tf_op jit(solution)/shard_map/ppermute | solution.py:49
  73.1 12.0 %collective-permute-start.4 = (bf16[128,2560]{1,0:T(8,128)(2,1)S(1)}, bf16[128,2560]{1,0:T(8,128)(2,1)S(1)}, u32[]{:S(2)}, u32[]{:S(2)}) collective-permute-start(bf16[128,2560]{1,0:T(8,128)(2,1)S(1)} %pad_maximum_fusion), channel_id=1, source_target_pairs={{0,96},{1,97},{2,98},{3,99},{4,36},{5,37},{6,38},{7,39},{8,104},{9... | collective-permute-start | bytes 1966088 | tf_op jit(solution)/shard_map/ppermute | solution.py:49
  85.1 14.0 %collective-permute-start.19 = (bf16[128,2560]{1,0:T(8,128)(2,1)S(1)}, bf16[128,2560]{1,0:T(8,128)(2,1)S(1)}, u32[]{:S(2)}, u32[]{:S(2)}) collective-permute-start(bf16[128,2560]{1,0:T(8,128)(2,1)S(1)} %pad_maximum_fusion.5.refs_1_), channel_id=1, source_target_pairs={{0,32},{1,33},{2,34},{3,35},{4,100},{5,101},{6,102},{7,103},{8,40}... | collective-permute-start | bytes 1966088 | tf_op jit(solution)/shard_map/ppermute | solution.py:49
  85.5 5.2 %collective-permute-start.14 = (bf16[240,2560]{1,0:T(8,128)(2,1)S(1)}, bf16[240,2560]{1,0:T(8,128)(2,1)S(1)}, u32[]{:S(2)}, u32[]{:S(2)}) collective-permute-start(bf16[240,2560]{1,0:T(8,128)(2,1)S(1)} %collective-permute-done.10.refs_7_), channel_id=1, source_target_pairs={{0,4},{1,5},{2,6},{3,7},{4,0},{5,1},{6,2},{7,3},{8,12},{9,13},{10,... | collective-permute-start | bytes 3686408 | tf_op jit(solution)/shard_map/ppermute | solution.py:49
  85.6 13.5 %collective-permute-start.18 = (bf16[128,2560]{1,0:T(8,128)(2,1)S(1)}, bf16[128,2560]{1,0:T(8,128)(2,1)S(1)}, u32[]{:S(2)}, u32[]{:S(2)}) collective-permute-start(bf16[128,2560]{1,0:T(8,128)(2,1)S(1)} %pad_maximum_fusion.2.refs_0_), channel_id=1, source_target_pairs={{0,3},{1,2},{2,1},{3,0},{4,5},{5,4},{6,7},{7,6},{8,11},{9,10},{10,... | collective-permute-start | bytes 1966088 | tf_op jit(solution)/shard_map/ppermute | solution.py:49
  88.1 17.9 %collective-permute-start.17 = (bf16[128,2560]{1,0:T(8,128)(2,1)S(1)}, bf16[128,2560]{1,0:T(8,128)(2,1)S(1)}, u32[]{:S(2)}, u32[]{:S(2)}) collective-permute-start(bf16[128,2560]{1,0:T(8,128)(2,1)S(1)} %pad_maximum_fusion.7.refs_3_), channel_id=1, source_target_pairs={{0,32},{1,33},{2,34},{3,35},{4,100},{5,101},{6,102},{7,103},{8,40}... | collective-permute-start | bytes 1966088 | tf_op jit(solution)/shard_map/ppermute | solution.py:49
  89.7 18.2 %collective-permute-start.16 = (bf16[128,2560]{1,0:T(8,128)(2,1)S(1)}, bf16[128,2560]{1,0:T(8,128)(2,1)S(1)}, u32[]{:S(2)}, u32[]{:S(2)}) collective-permute-start(bf16[128,2560]{1,0:T(8,128)(2,1)S(1)} %pad_maximum_fusion.6.refs_2_), channel_id=1, source_target_pairs={{0,3},{1,2},{2,1},{3,0},{4,5},{5,4},{6,7},{7,6},{8,11},{9,10},{10,... | collective-permute-start | bytes 1966088 | tf_op jit(solution)/shard_map/ppermute | solution.py:49
  102.8 10.7 %collective-permute-start.20 = (bf16[128,2560]{1,0:T(8,128)(2,1)S(1)}, bf16[128,2560]{1,0:T(8,128)(2,1)S(1)}, u32[]{:S(2)}, u32[]{:S(2)}) collective-permute-start(bf16[128,2560]{1,0:T(8,128)(2,1)S(1)} %get-tuple-element.20), channel_id=1, source_target_pairs={{0,32},{1,33},{2,34},{3,35},{4,100},{5,101},{6,102},{7,103},{8,40}... | collective-permute-start | bytes 1966088 | tf_op jit(solution)/shard_map/ppermute | solution.py:49
  104.3 16.2 %collective-permute-start.15 = (bf16[128,2560]{1,0:T(8,128)(2,1)S(1)}, bf16[128,2560]{1,0:T(8,128)(2,1)S(1)}, u32[]{:S(2)}, u32[]{:S(2)}) collective-permute-start(bf16[128,2560]{1,0:T(8,128)(2,1)S(1)} %get-tuple-element.16), channel_id=1, source_target_pairs={{0,32},{1,33},{2,34},{3,35},{4,100},{5,101},{6,102},{7,103},{8,40}... | collective-permute-start | bytes 1966088 | tf_op jit(solution)/shard_map/ppermute | solution.py:49
  105.9 11.2 %collective-permute-start.25 = (bf16[128,2560]{1,0:T(8,128)(2,1)S(1)}, bf16[128,2560]{1,0:T(8,128)(2,1)S(1)}, u32[]{:S(2)}, u32[]{:S(2)}) collective-permute-start(bf16[128,2560]{1,0:T(8,128)(2,1)S(1)} %get-tuple-element.24), channel_id=1, source_target_pairs={{0,1},{1,0},{2,3},{3,2},{4,7},{5,6},{6,5},{7,4},{8,9},{9,8},{10,11... | collective-permute-start | bytes 1966088 | tf_op jit(solution)/shard_map/ppermute | solution.py:49
  105.9 26.3 %collective-permute-start.24 = (bf16[128,2560]{1,0:T(8,128)(2,1)S(1)}, bf16[128,2560]{1,0:T(8,128)(2,1)S(1)}, u32[]{:S(2)}, u32[]{:S(2)}) collective-permute-start(bf16[128,2560]{1,0:T(8,128)(2,1)S(1)} %get-tuple-element.22), channel_id=1, source_target_pairs={{0,1},{1,0},{2,3},{3,2},{4,7},{5,6},{6,5},{7,4},{8,9},{9,8},{10,11... | collective-permute-start | bytes 1966088 | tf_op jit(solution)/shard_map/ppermute | solution.py:49
  113.7 17.3 %collective-permute-start.21 = (bf16[128,2560]{1,0:T(8,128)(2,1)S(1)}, bf16[128,2560]{1,0:T(8,128)(2,1)S(1)}, u32[]{:S(2)}, u32[]{:S(2)}) collective-permute-start(bf16[128,2560]{1,0:T(8,128)(2,1)S(1)} %add_convert_fusion.1), channel_id=1, source_target_pairs={{0,3},{1,2},{2,1},{3,0},{4,5},{5,4},{6,7},{7,6},{8,11},{9,10},{10,... | collective-permute-start | bytes 1966088 | tf_op jit(solution)/shard_map/ppermute | solution.py:49
  117.2 15.0 %collective-permute-start.26 = (bf16[128,2560]{1,0:T(8,128)(2,1)S(1)}, bf16[128,2560]{1,0:T(8,128)(2,1)S(1)}, u32[]{:S(2)}, u32[]{:S(2)}) collective-permute-start(bf16[128,2560]{1,0:T(8,128)(2,1)S(1)} %add_convert_fusion), channel_id=1, source_target_pairs={{0,32},{1,33},{2,34},{3,35},{4,100},{5,101},{6,102},{7,103},{8,40}... | collective-permute-start | bytes 1966088 | tf_op jit(solution)/shard_map/ppermute | solution.py:49
  131.2 8.4 %collective-permute-start.22 = (bf16[64,2560]{1,0:T(8,128)(2,1)S(1)}, bf16[64,2560]{1,0:T(8,128)(2,1)S(1)}, u32[]{:S(2)}, u32[]{:S(2)}) collective-permute-start(bf16[64,2560]{1,0:T(8,128)(2,1)S(1)} %slice.138), channel_id=1, source_target_pairs={{0,96},{1,97},{2,98},{3,99},{4,36},{5,37},{6,38},{7,39},{8,104},{9... | collective-permute-start | bytes 983048 | tf_op jit(solution)/shard_map/ppermute | solution.py:49
  132.5 8.6 %collective-permute-start.27 = (bf16[64,2560]{1,0:T(8,128)(2,1)S(1)}, bf16[64,2560]{1,0:T(8,128)(2,1)S(1)}, u32[]{:S(2)}, u32[]{:S(2)}) collective-permute-start(bf16[64,2560]{1,0:T(8,128)(2,1)S(1)} %slice.137), channel_id=1, source_target_pairs={{0,3},{1,2},{2,1},{3,0},{4,5},{5,4},{6,7},{7,6},{8,11},{9,10},{10,... | collective-permute-start | bytes 983048 | tf_op jit(solution)/shard_map/ppermute | solution.py:49
  139.6 5.4 %collective-permute-start.23 = (bf16[32,2560]{1,0:T(8,128)(2,1)S(1)}, bf16[32,2560]{1,0:T(8,128)(2,1)S(1)}, u32[]{:S(2)}, u32[]{:S(2)}) collective-permute-start(bf16[32,2560]{1,0:T(8,128)(2,1)S(1)} %slice.141), channel_id=1, source_target_pairs={{0,1},{1,0},{2,3},{3,2},{4,7},{5,6},{6,5},{7,4},{8,9},{9,8},{10,11... | collective-permute-start | bytes 491528 | tf_op jit(solution)/shard_map/ppermute | solution.py:49
  141.2 6.9 %collective-permute-start.28 = (bf16[32,2560]{1,0:T(8,128)(2,1)S(1)}, bf16[32,2560]{1,0:T(8,128)(2,1)S(1)}, u32[]{:S(2)}, u32[]{:S(2)}) collective-permute-start(bf16[32,2560]{1,0:T(8,128)(2,1)S(1)} %slice.140), channel_id=1, source_target_pairs={{0,96},{1,97},{2,98},{3,99},{4,36},{5,37},{6,38},{7,39},{8,104},{9... | collective-permute-start | bytes 491528 | tf_op jit(solution)/shard_map/ppermute | solution.py:49
